TPU v7x, 1024 devices: a whole 4x4x32 slice. The times are simulated.
1024 devices in a mesh: seq: 16 (over x, y), row: 8 (over z_hi, core), col: 8 (over z_lo).
Axes of the slice: x: 4, y: 4, z: 32 (z_hi: 4, z_lo: 8; z = z_hi * 8 + z_lo), core: 2. Of those that a mesh axis runs over, the one named last changes fastest.
Arguments:
- query_rows: bfloat16 [2048, 16384], P('seq', ('row', 'col')), may hold values from -9.5625 to 9.5625
- key_rows: bfloat16 [2048, 16384], P('seq', ('row', 'col')), may hold values from -16 to 16
- value_rows: bfloat16 [2048, 16384], P('seq', ('row', 'col')), may hold values from -6 to 6
- out_grad: bfloat16 [2048, 16384], P('seq', ('row', 'col')), may hold values from -6 to 6
- mix_pre: bfloat16 [128, 128], replicated, may hold values from -0.3 to 1.3
- mix_post: bfloat16 [128, 128], replicated, may hold values from -0.3 to 1.3
- block_order: int32 [16], replicated, may hold values from 0 to 15, each once
Outputs:
- attention_out: bfloat16 [2048, 16384], P('seq', ('row', 'col'))
- grad_query: bfloat16 [2048, 16384], P('seq', ('row', 'col'))
- grad_key: bfloat16 [2048, 16384], P('seq', ('row', 'col'))
- grad_value: bfloat16 [2048, 16384], P('seq', ('row', 'col'))
Inputs may be any that keep to these rules, and one draw needn't show every extreme that they name: block_order holds every number below 16 once.
All inputs are finite; a program needn't handle non-finite values.
Results may differ from a plain program's by a relative error of at most 0.012.
Values may be sent and summed in bfloat16 or wider, within the bound.
No kernel may reach another device: no remote copies, remote signals or barrier semaphores. Data moves between devices by JAX's collectives and lax.ppermute only.
A program may use at most 32 MiB of HBM per device.

v0:
```python
import jax
import jax.numpy as jnp
from jax import lax
from jax.sharding import PartitionSpec as P

DH = 128


logit_cap = 10.0


def body(query_rows, key_rows, value_rows, out_grad, mix_pre, mix_post, block_order):
    seq_count = lax.axis_size("seq")
    row_count = lax.axis_size("row")
    col_count = lax.axis_size("col")
    local_rows = query_rows.shape[0]
    heads_local = query_rows.shape[1] // DH
    heads_all = mix_pre.shape[0]
    scaling = DH ** (-0.5)
    sub_rows = local_rows // (row_count * col_count)
    query_heads = query_rows.reshape(local_rows, heads_local, DH)
    upstream = out_grad.reshape(local_rows, heads_local, DH)
    key_all, value_all = (
        lax.all_gather(key_rows, "seq", axis=0, tiled=True),
        lax.all_gather(value_rows, "seq", axis=0, tiled=True),
    )
    seq_len = key_all.shape[0]
    key_heads = key_all.reshape(seq_len, heads_local, DH)
    value_heads = value_all.reshape(seq_len, heads_local, DH)
    own_block = jnp.sum(
        jnp.where(jnp.arange(seq_count, dtype=jnp.int32) == lax.axis_index("seq"), block_order, 0)
    )
    key_place = jnp.repeat(block_order, local_rows) * local_rows + jnp.tile(
        jnp.arange(local_rows, dtype=jnp.int32), seq_count
    )
    scores = (
        (
            jnp.einsum("qhd,khd->qhk", query_heads, key_heads, preferred_element_type=jnp.float32)
            * scaling
        )
        .astype(jnp.bfloat16)
        .reshape(local_rows, -1)
    )
    grad_post = (
        jnp.einsum("qhd,khd->qhk", upstream, value_heads, preferred_element_type=jnp.float32)
        .astype(jnp.bfloat16)
        .reshape(local_rows, -1)
    )
    sub_block = lax.axis_index("row") * col_count + lax.axis_index("col")
    mixed_scores, mixed_grad = (
        lax.all_to_all(scores, ("row", "col"), split_axis=0, concat_axis=1, tiled=True),
        lax.all_to_all(grad_post, ("row", "col"), split_axis=0, concat_axis=1, tiled=True),
    )
    query_place = (
        own_block * local_rows + sub_block * sub_rows + jnp.arange(sub_rows, dtype=jnp.int32)
    )
    mixed_view = mixed_scores.reshape(sub_rows, heads_all, seq_len)
    grad_view = mixed_grad.reshape(sub_rows, heads_all, seq_len)
    block_width = 512
    block_count = seq_len // block_width

    def recompute(offset):
        score_block = lax.dynamic_slice_in_dim(mixed_view, offset, block_width, 2)
        mixed_logits = jnp.einsum(
            "gh,qhk->qgk", mix_pre, score_block, preferred_element_type=jnp.float32
        )
        capped = logit_cap * jnp.tanh(mixed_logits / logit_cap)
        near_keys = lax.dynamic_slice_in_dim(key_place, offset, block_width, 0)
        allowed = near_keys[None, None, :] <= query_place[:, None, None]
        weights = jnp.where(allowed, jnp.exp(capped), 0.0)
        return (capped, weights)

    def add_total(number, running):
        capped, weights = recompute(number * block_width)
        return running + jnp.sum(weights, axis=2)

    totals = lax.fori_loop(0, block_count, add_total, jnp.zeros((sub_rows, heads_all), jnp.float32))

    def probs_at(offset):
        capped, weights = recompute(offset)
        return (capped, weights / totals[:, :, None])

    def forward_block(number, state_pair):
        post_all, rowdot = state_pair
        offset = number * block_width
        capped, prob_block = probs_at(offset)
        post_block = jnp.einsum(
            "gh,qhk->qgk",
            mix_post,
            prob_block.astype(jnp.bfloat16),
            preferred_element_type=jnp.float32,
        ).astype(jnp.bfloat16)
        post_all = lax.dynamic_update_slice_in_dim(post_all, post_block, offset, 2)
        grad_block = lax.dynamic_slice_in_dim(grad_view, offset, block_width, 2)
        grad_probs = jnp.einsum(
            "gh,qgk->qhk", mix_post, grad_block, preferred_element_type=jnp.float32
        )
        return (post_all, rowdot + jnp.sum(prob_block * grad_probs, axis=2))

    post_start = jnp.zeros((sub_rows, heads_all, seq_len), jnp.bfloat16)
    post_all, rowdot = lax.fori_loop(
        0, block_count, forward_block, (post_start, jnp.zeros((sub_rows, heads_all), jnp.float32))
    )

    def backward_block(number, grad_all):
        offset = number * block_width
        capped, prob_block = probs_at(offset)
        grad_block = lax.dynamic_slice_in_dim(grad_view, offset, block_width, 2)
        grad_probs = jnp.einsum(
            "gh,qgk->qhk", mix_post, grad_block, preferred_element_type=jnp.float32
        )
        grad_capped = prob_block * (grad_probs - rowdot[:, :, None])
        grad_mixed = (grad_capped * (1.0 - (capped / logit_cap) ** 2)).astype(jnp.bfloat16)
        grad_scores = (
            scaling
            * jnp.einsum("gh,qgk->qhk", mix_pre, grad_mixed, preferred_element_type=jnp.float32)
        ).astype(jnp.bfloat16)
        return lax.dynamic_update_slice_in_dim(grad_all, grad_scores, offset, 2)

    grad_all = lax.fori_loop(
        0, block_count, backward_block, jnp.zeros((sub_rows, heads_all, seq_len), jnp.bfloat16)
    )
    post_flat = post_all.reshape(sub_rows, -1)
    grad_flat = grad_all.reshape(sub_rows, -1)
    post_heads, score_heads = (
        lax.all_to_all(post_flat, ("row", "col"), split_axis=1, concat_axis=0, tiled=True),
        lax.all_to_all(grad_flat, ("row", "col"), split_axis=1, concat_axis=0, tiled=True),
    )
    post_local = post_heads.reshape(local_rows, heads_local, seq_len)
    score_local = score_heads.reshape(local_rows, heads_local, seq_len)
    attended = (
        jnp.einsum("qhk,khd->qhd", post_local, value_heads, preferred_element_type=jnp.float32)
        .astype(jnp.bfloat16)
        .reshape(local_rows, -1)
    )
    grad_query = (
        jnp.einsum("qhk,khd->qhd", score_local, key_heads, preferred_element_type=jnp.float32)
        .astype(jnp.bfloat16)
        .reshape(local_rows, -1)
    )
    key_term = jnp.einsum(
        "qhk,qhd->khd", score_local, query_heads, preferred_element_type=jnp.float32
    ).reshape(lax.axis_size("seq") * local_rows, -1)
    value_term = jnp.einsum(
        "qhk,qhd->khd", post_local, upstream, preferred_element_type=jnp.float32
    ).reshape(lax.axis_size("seq") * local_rows, -1)
    summed = lax.psum_scatter(
        jnp.concatenate([key_term, value_term], axis=1).astype(jnp.bfloat16),
        "seq",
        scatter_dimension=0,
        tiled=True,
    ).astype(jnp.float32)
    half_cols = heads_local * DH
    grad_key = summed[:, :half_cols].astype(jnp.bfloat16)
    grad_value = summed[:, half_cols:].astype(jnp.bfloat16)
    return (attended, grad_query, grad_key, grad_value)


def solution(mesh):
    return jax.shard_map(
        body,
        mesh=mesh,
        in_specs=(
            P("seq", ("row", "col")),
            P("seq", ("row", "col")),
            P("seq", ("row", "col")),
            P("seq", ("row", "col")),
            P(),
            P(),
            P(),
        ),
        out_specs=(
            P("seq", ("row", "col")),
            P("seq", ("row", "col")),
            P("seq", ("row", "col")),
            P("seq", ("row", "col")),
        ),
        check_vma=False,
    )
```

profile of v0, /device:TPU:2, one launch (start us, length us, event | category | flops | bytes accessed | tf_op | source)
XLA Modules:
  0.0 707.3 jit_solution(13398815594849698895)
XLA Ops:
  7.2 1.6 copy.56
  8.8 1.0 copy.86
  9.8 89.1 %all-gather.5.cloned.1.call-done = bf16[2048,256]{0,1:T(8,128)(2,1)} async-done(((bf16[128,256]{0,1:T(8,128)(2,1)}), bf16[2048,256]{0,1:T(8,128)(2,1)}) %all-gather.5.cloned.1.call-update) | async-done | bytes 1048592 | tf_op jit(solution)/shard_map/all_gather | solution.py:25
  98.9 1.8 fusion.63
  100.7 1.0 copy.59
  101.7 1.6 all_to_all.51
  103.3 23.5 %all-to-all-start.1 = ((bf16[64,2,4096]{2,1,0:T(2,128)(2,1)}), bf16[64,2,4096]{2,1,0:T(2,128)(2,1)S(1)}, u32[]{:S(2)}, u32[]{:S(2)}) async-start(bf16[64,2,4096]{2,1,0:T(2,128)(2,1)} %all_to_all.51), calls=%async_computation.1 | async-start | bytes 2097152 | tf_op jit(solution)/shard_map/all_to_all | solution.py:52
  127.8 82.0 %all-gather.3.cloned.1.call-done = bf16[2048,256]{0,1:T(8,128)(2,1)} async-done(((bf16[128,256]{0,1:T(8,128)(2,1)}), bf16[2048,256]{0,1:T(8,128)(2,1)}) %all-gather.3.cloned.1.call-update) | async-done | bytes 1048592 | tf_op jit(solution)/shard_map/all_gather | solution.py:24
  209.8 1.8 fusion.64
  211.5 1.0 copy.53
  212.5 1.6 all_to_all.48
  214.2 23.4 %all-to-all-done.1 = bf16[64,2,4096]{2,1,0:T(2,128)(2,1)S(1)} async-done(((bf16[64,2,4096]{2,1,0:T(2,128)(2,1)}), bf16[64,2,4096]{2,1,0:T(2,128)(2,1)S(1)}, u32[]{:S(2)}, u32[]{:S(2)}) %all-to-all-start.1) | async-done | bytes 1048608 | tf_op jit(solution)/shard_map/all_to_all | solution.py:52
  237.5 4.7 all-to-all-start
  244.2 1.2 reshape.166
  245.4 1.6 copy.62
  247.0 105.8 %all-to-all-done = bf16[64,2,4096]{2,1,0:T(2,128)(2,1)S(1)} async-done(((bf16[64,2,4096]{2,1,0:T(2,128)(2,1)}), bf16[64,2,4096]{2,1,0:T(2,128)(2,1)S(1)}, u32[]{:S(2)}, u32[]{:S(2)}) %all-to-all-start) | async-done | bytes 1048608 | tf_op jit(solution)/shard_map/all_to_all | solution.py:51
  353.5 1.2 reshape.163
  354.6 1.6 copy.61
  356.3 2.2 while.47
  358.5 1.1 broadcast.173.clone2
  359.6 8.3 %while.48 = (s32[]{:T(128)}, bf16[2,128,2048]{2,1,0:T(8,128)(2,1)}, f32[2,128]{1,0:T(2,128)S(1)}, s32[2048]{0:T(1024)S(1)}, bf16[2,128,2048]{1,2,0:T(8,128)(2,1)...) while((s32[]{:T(128)}, bf16[2,128,2048]{2,1,0:T(8,128)(2,1)}, ...), condition=%wide.region_6.7_spmd.clone, body=%wide.region_4.6_spmd.clone.sunk | while | flops 101713160 | bytes 3520745 | solution.py:101
  360.9 0.8 constant_dynamic-update-slice_fusion.5
  365.0 0.8 constant_dynamic-update-slice_fusion.5
  367.0 0.8 constant_dynamic-update-slice_fusion.5
  367.8 1.4 all_to_all.54
  369.2 2.1 copy.64
  371.3 5.7 all-to-all-start.2
  377.0 1.1 broadcast.173.clone
  378.1 6.9 while.46
  379.1 0.8 constant_dynamic-update-slice_fusion.4
  384.2 0.8 constant_dynamic-update-slice_fusion.4
  385.0 1.4 all_to_all.57
  386.4 2.1 copy.69
  388.5 98.8 %all-to-all-done.2 = bf16[2,64,4096]{2,0,1:T(2,128)(2,1)} async-done(((bf16[2,64,4096]{2,0,1:T(2,128)(2,1)}), bf16[2,64,4096]{2,0,1:T(2,128)(2,1)}, u32[]{:S(2)}, u32[]{:S(2)}) %all-to-all-start.2) | async-done | bytes 1048608 | tf_op jit(solution)/shard_map/all_to_all | solution.py:126
  487.3 4.7 all-to-all-start.3
  492.1 3.7 reshape.167
  495.7 0.9 convolution_convert_fusion.1
  496.6 1.3 copy.76
  497.9 104.7 %all-to-all-done.3 = bf16[2,64,4096]{2,0,1:T(2,128)(2,1)S(1)} async-done(((bf16[2,64,4096]{2,0,1:T(2,128)(2,1)}), bf16[2,64,4096]{2,0,1:T(2,128)(2,1)S(1)}, u32[]{:S(2)}, u32[]{:S(2)}) %all-to-all-start.3) | async-done | bytes 1048608 | tf_op jit(solution)/shard_map/all_to_all | solution.py:127
  602.7 0.8 reshape.169
  603.5 0.9 convolution_convert_fusion.2
  604.3 1.3 copy.75
  605.7 3.0 pad_maximum_fusion
  608.7 1.2 copy-done.1
  610.5 0.8 copy.77
  611.2 1.8 convolution_convert_fusion.4
  613.8 85.5 %reduce-scatter.2.cloned.1.call-done = bf16[128,512]{1,0:T(8,128)(2,1)} async-done(((bf16[2048,512]{1,0:T(8,128)(2,1)}), bf16[128,512]{1,0:T(8,128)(2,1)}) %reduce-scatter.2.cloned.1.call-update) | async-done | bytes 131088 | tf_op jit(solution)/shard_map/reduce_scatter | solution.py:147
  699.2 1.5 fusion.70
  (106 shorter events, 17.3 us)
Async XLA Ops:
  7.2 91.7 %all-gather.5.cloned.1.call-start = ((), (), s32[]{:S(2)}) async-start(), calls=%async_computation.6 | async-start | bytes 1114112 | tf_op jit(solution)/shard_map/all_gather | solution.py:25
  101.7 25.3 %copy-start.3 = (bf16[128,256]{1,0:T(8,128)(2,1)S(1)}, bf16[128,256]{1,0:T(8,128)(2,1)}, u32[]{:S(2)}) copy-start(bf16[128,256]{1,0:T(8,128)(2,1)} %param.14) | copy-start | bytes 196612
  101.7 26.0 %copy-start.4 = (bf16[128,256]{1,0:T(8,128)(2,1)S(1)}, bf16[128,256]{1,0:T(8,128)(2,1)}, u32[]{:S(2)}) copy-start(bf16[128,256]{1,0:T(8,128)(2,1)} %param.13) | copy-start | bytes 196612
  103.3 134.2 %all-to-all-start.1 = ((bf16[64,2,4096]{2,1,0:T(2,128)(2,1)}), bf16[64,2,4096]{2,1,0:T(2,128)(2,1)S(1)}, u32[]{:S(2)}, u32[]{:S(2)}) async-start(bf16[64,2,4096]{2,1,0:T(2,128)(2,1)} %all_to_all.51), calls=%async_computation.1 | async-start | bytes 2097152 | tf_op jit(solution)/shard_map/all_to_all | solution.py:52
  126.9 82.9 %all-gather.3.cloned.1.call-start = ((), (), s32[]{:S(2)}) async-start(), calls=%async_computation.5 | async-start | bytes 1114112 | tf_op jit(solution)/shard_map/all_gather | solution.py:24
  212.5 29.7 %copy-start.5 = (s32[16]{0:T(128)S(1)}, s32[16]{0:T(128)}, u32[]{:S(2)}) copy-start(s32[16]{0:T(128)} %param.19) | copy-start | bytes 196
  237.5 115.3 %all-to-all-start = ((bf16[64,2,4096]{2,1,0:T(2,128)(2,1)}), bf16[64,2,4096]{2,1,0:T(2,128)(2,1)S(1)}, u32[]{:S(2)}, u32[]{:S(2)}) async-start(bf16[64,2,4096]{2,1,0:T(2,128)(2,1)} %all_to_all.48), calls=%async_computation | async-start | bytes 2097152 | tf_op jit(solution)/shard_map/all_to_all | solution.py:51
  353.4 2.8 copy-start.2
  356.3 3.3 copy-start
  371.3 116.0 %all-to-all-start.2 = ((bf16[2,64,4096]{2,0,1:T(2,128)(2,1)}), bf16[2,64,4096]{2,0,1:T(2,128)(2,1)}, u32[]{:S(2)}, u32[]{:S(2)}) async-start(bf16[2,64,4096]{2,0,1:T(2,128)(2,1)} %copy.64), calls=%async_computation.2 | async-start | bytes 2097152 | tf_op jit(solution)/shard_map/all_to_all | solution.py:126
  487.3 115.3 %all-to-all-start.3 = ((bf16[2,64,4096]{2,0,1:T(2,128)(2,1)}), bf16[2,64,4096]{2,0,1:T(2,128)(2,1)S(1)}, u32[]{:S(2)}, u32[]{:S(2)}) async-start(bf16[2,64,4096]{2,0,1:T(2,128)(2,1)} %copy.69), calls=%async_computation.3 | async-start | bytes 2097152 | tf_op jit(solution)/shard_map/all_to_all | solution.py:127
  492.0 207.2 %reduce-scatter.2.cloned.1.call-start = ((), (), s32[]{:S(2)}) async-start(), calls=%async_computation.7 | async-start | bytes 2228224 | tf_op jit(solution)/shard_map/reduce_scatter | solution.py:147
  608.7 1.2 copy-start.1
Sparse Core Ops, SparseCore 0:
  12.7 86.1 all-gather.4
  132.4 77.3 all-gather.2
  608.8 90.3 reduce-scatter.1
where the time goes:
time: 708 us; the launch traced here: 707 us
  waiting for transfers between devices  589 us (83%)
  local copies, waits for them, and re-layouts  44.1 us (6%)
  starting transfers between devices  38.7 us (5%)
  matrix products  15.3 us (2%)
  between operations  14.7 us (2%)
    all_to_all x1, waiting for transfers between devices, body(): lax.all_to_all(scores, ('row', 'col'), split_axis=0, concat_axis=1, tiled...  106 us
    all_to_all x1, waiting for transfers between devices, body(): lax.all_to_all(grad_flat, ('row', 'col'), split_axis=1, concat_axis=0, ti...  105 us
    all_to_all x1, waiting for transfers between devices, body(): lax.all_to_all(post_flat, ('row', 'col'), split_axis=1, concat_axis=0, ti...  98.8 us
    all_gather x1, waiting for transfers between devices, body(): lax.all_gather(value_rows, 'seq', axis=0, tiled=True)  89.1 us
    reduce_scatter x1, waiting for transfers between devices, body(): lax.psum_scatter(jnp.concatenate([key_term, value_term], axis=1).astype(j...  85.5 us
    all_gather x1, waiting for transfers between devices, body(): lax.all_gather(key_rows, 'seq', axis=0, tiled=True)  82 us
    all_to_all x1, starting transfers between devices, body(): lax.all_to_all(grad_post, ('row', 'col'), split_axis=0, concat_axis=1, ti...  23.5 us
    all_to_all x1, waiting for transfers between devices, body(): lax.all_to_all(grad_post, ('row', 'col'), split_axis=0, concat_axis=1, ti...  23.4 us
  transfers between devices with their start and end apart: 7, of which 7 were waited for; matrix products, arithmetic and copies ran while one was open for 4% of the time, Pallas kernels for 0%

commit v1 on v0

v1 whole, which is shorter than its diff:
```python
import jax
import jax.numpy as jnp
from jax import lax
from jax.sharding import PartitionSpec as P

DH = 128


logit_cap = 10.0

HEAD_AXES = ("row", "col")


def body(query_rows, key_rows, value_rows, out_grad, mix_pre, mix_post, block_order):
    blocks = lax.axis_size("seq")
    owners = lax.axis_size("row") * lax.axis_size("col")
    rows, width = query_rows.shape
    heads_local = width // DH
    heads_all = mix_pre.shape[0]
    scaling = DH ** (-0.5)
    strip = rows // blocks
    half = blocks // 2
    span = (blocks + 1) * rows
    seq_len = blocks * rows
    seq_index = lax.axis_index("seq")

    key_value = jnp.concatenate([key_rows, value_rows], axis=1)
    query_grad = jnp.concatenate([query_rows, out_grad], axis=1).reshape(blocks, strip, 2 * width)
    sent = jnp.concatenate(
        [jnp.broadcast_to(key_value[None], (blocks, rows, 2 * width)), query_grad], axis=1
    )
    received = lax.all_to_all(sent, "seq", split_axis=0, concat_axis=0, tiled=True)
    numbers = jnp.arange(blocks, dtype=jnp.int32)
    stored_at = jnp.sum(
        jnp.where(block_order[None, :] == numbers[:, None], numbers[None, :], 0), axis=1
    )
    by_place = jnp.take(received, stored_at, axis=0)
    key_value_all = by_place[:, :rows].reshape(seq_len, 2, heads_local, DH)
    query_grad_all = by_place[:, rows:].reshape(rows, 2, heads_local, DH)
    key_heads, value_heads = key_value_all[:, 0], key_value_all[:, 1]
    query_heads, upstream = query_grad_all[:, 0], query_grad_all[:, 1]

    def pack(dense):
        view = dense.reshape(heads_local, blocks, strip, seq_len)
        parts = []
        for c in range(half):
            near = view[:, c, :, : rows * (c + 1)]
            far = view[:, blocks - 1 - c, :, : rows * (blocks - c)]
            parts.append(jnp.concatenate([near, far], axis=2))
        return jnp.concatenate(parts, axis=1)

    def unpack(packed):
        view = packed.reshape(-1, half, strip, span)
        parts = []
        for p in range(blocks):
            if p < half:
                piece = view[:, p, :, : rows * (p + 1)]
            else:
                piece = view[:, blocks - 1 - p, :, rows * (blocks - p) :]
            parts.append(jnp.pad(piece, ((0, 0), (0, 0), (0, seq_len - rows * (p + 1)))))
        return jnp.concatenate(parts, axis=1)

    scores = (
        jnp.einsum("qhd,khd->hqk", query_heads, key_heads, preferred_element_type=jnp.float32)
        * scaling
    ).astype(jnp.bfloat16)
    grad_post = jnp.einsum(
        "qhd,khd->hqk", upstream, value_heads, preferred_element_type=jnp.float32
    ).astype(jnp.bfloat16)
    outgoing = jnp.concatenate([pack(scores), pack(grad_post)], axis=0)
    incoming = lax.all_to_all(outgoing, HEAD_AXES, split_axis=1, concat_axis=1, tiled=True)
    incoming = incoming.reshape(2, heads_all, span)

    def reorder(mix):
        view = mix.reshape(owners, heads_local, owners, heads_local)
        return view.transpose(1, 0, 3, 2).reshape(heads_all, heads_all)

    pre, post = reorder(mix_pre), reorder(mix_post)
    own = lax.axis_index(HEAD_AXES)
    pair, line = own // strip, own % strip
    bound = rows * (pair + 1)
    lane = lax.broadcasted_iota(jnp.int32, (1, span), 1)
    is_near = lane < bound
    key_place = jnp.where(is_near, lane, lane - bound)
    query_place = (
        jnp.where(is_near, pair, blocks - 1 - pair) * rows + seq_index * strip + line
    )
    allowed = key_place <= query_place

    def row_sum(values):
        near = jnp.sum(jnp.where(is_near, values, 0.0), axis=1, keepdims=True)
        far = jnp.sum(jnp.where(is_near, 0.0, values), axis=1, keepdims=True)
        return near, far

    mixed = jnp.dot(pre, incoming[0], preferred_element_type=jnp.float32)
    squashed = jnp.tanh(mixed / logit_cap)
    weights = jnp.where(allowed, jnp.exp(logit_cap * squashed), 0.0)
    near_total, far_total = row_sum(weights)
    probs = weights * jnp.where(is_near, 1.0 / near_total, 1.0 / far_total)
    post_mixed = jnp.dot(
        post, probs.astype(jnp.bfloat16), preferred_element_type=jnp.float32
    ).astype(jnp.bfloat16)
    grad_probs = jnp.einsum("gh,gk->hk", post, incoming[1], preferred_element_type=jnp.float32)
    near_dot, far_dot = row_sum(probs * grad_probs)
    grad_capped = probs * (grad_probs - jnp.where(is_near, near_dot, far_dot))
    grad_mixed = (grad_capped * (1.0 - squashed * squashed)).astype(jnp.bfloat16)
    grad_scores = (
        scaling * jnp.einsum("gh,gk->hk", pre, grad_mixed, preferred_element_type=jnp.float32)
    ).astype(jnp.bfloat16)

    outgoing = jnp.concatenate([post_mixed, grad_scores], axis=0).reshape(
        2 * heads_local, owners, span
    )
    incoming = lax.all_to_all(outgoing, HEAD_AXES, split_axis=1, concat_axis=1, tiled=True)
    post_dense = unpack(incoming[:heads_local])
    score_dense = unpack(incoming[heads_local:])

    def rounded(spec, left, right):
        return jnp.einsum(spec, left, right, preferred_element_type=jnp.float32).astype(
            jnp.bfloat16
        )

    attended = rounded("hqk,khd->qhd", post_dense, value_heads)
    grad_query = rounded("hqk,khd->qhd", score_dense, key_heads)
    key_term = rounded("hqk,qhd->khd", score_dense, query_heads)
    value_term = rounded("hqk,qhd->khd", post_dense, upstream)
    terms = jnp.stack([key_term, value_term], axis=1).reshape(blocks, rows, 2 * width)
    results = jnp.stack([attended, grad_query], axis=1).reshape(blocks, strip, 2 * width)
    sent = jnp.take(jnp.concatenate([terms, results], axis=1), block_order, axis=0)
    received = lax.all_to_all(sent, "seq", split_axis=0, concat_axis=0, tiled=True)
    summed = jnp.sum(received[:, :rows].astype(jnp.float32), axis=0).astype(jnp.bfloat16)
    results = received[:, rows:].reshape(rows, 2 * width)
    return (results[:, :width], results[:, width:], summed[:, :width], summed[:, width:])


def solution(mesh):
    spread = P("seq", HEAD_AXES)
    return jax.shard_map(
        body,
        mesh=mesh,
        in_specs=(spread, spread, spread, spread, P(), P(), P()),
        out_specs=(spread, spread, spread, spread),
        check_vma=False,
    )
```

time: 708 us -> 382 us (0.54)
  the two profiles are of different devices: /device:TPU:2 before, /device:TPU:32 now
where the time goes in v1:
time: 382 us; the launch traced here: 381 us
  waiting for transfers between devices  251 us (66%)
  starting transfers between devices  41.8 us (11%)
  local copies, waits for them, and re-layouts  34.2 us (9%)
  blocking collectives  32.7 us (9%)
  other arithmetic  12.9 us (3%)
  matrix products  6.26 us (2%)
    all_to_all x2, waiting for transfers between devices, body(): lax.all_to_all(outgoing, HEAD_AXES, split_axis=1, concat_axis=1, tiled=True)  219 us
    all_to_all x2, starting transfers between devices, body(): lax.all_to_all(outgoing, HEAD_AXES, split_axis=1, concat_axis=1, tiled=True)  34.6 us
    all_to_all x1, blocking collectives, body(): lax.all_to_all(sent, 'seq', split_axis=0, concat_axis=0, tiled=True)  32.7 us
    all_to_all x1, waiting for transfers between devices, body(): lax.all_to_all(sent, 'seq', split_axis=0, concat_axis=0, tiled=True)  31.9 us
    reshape x2, local copies, waits for them, and re-layouts, reorder(): view = mix.reshape(owners, heads_local, owners, heads_local)  9.07 us
  transfers between devices with their start and end apart: 3, of which 3 were waited for; matrix products, arithmetic and copies ran while one was open for 3% of the time, Pallas kernels for 0%

profile of v1, /device:TPU:32, one launch (start us, length us, event | category | flops | bytes accessed | tf_op | source)
XLA Modules:
  0.0 381.2 jit_solution(10652006290634978505)
XLA Ops:
  0.6 0.9 maximum_bitcast_fusion
  1.5 0.9 pad_maximum_fusion.5
  2.4 0.2 broadcast_in_dim.111
  2.6 1.5 pad_maximum_fusion
  4.1 7.2 %all-to-all-start = ((bf16[16,136,512]{2,1,0:T(8,128)(2,1)}), bf16[16,136,512]{2,1,0:T(8,128)(2,1)S(1)}, u32[]{:S(2)}, u32[]{:S(2)}) async-start(bf16[16,136,512]{2,1,0:T(8,128)(2,1)} %pad_maximum_fusion), calls=%async_computation | async-start | bytes 4456448 | tf_op jit(solution)/shard_map/all_to_all | solution.py:32
  11.5 31.9 %all-to-all-done = bf16[16,136,512]{2,1,0:T(8,128)(2,1)S(1)} async-done(((bf16[16,136,512]{2,1,0:T(8,128)(2,1)}), bf16[16,136,512]{2,1,0:T(8,128)(2,1)S(1)}, u32[]{:S(2)}, u32[]{:S(2)}) %all-to-all-start) | async-done | bytes 2228256 | tf_op jit(solution)/shard_map/all_to_all | solution.py:32
  43.4 2.1 gather_fusion
  45.4 1.9 broadcast_select_fusion.1
  47.3 1.5 slice.328
  48.9 2.5 reshape.136
  51.6 1.5 fusion.31
  53.1 0.4 fusion.8
  53.6 0.5 copy-done.2
  54.2 0.2 copy-done
  54.4 0.4 fusion.5
  55.5 0.2 slice-done
  57.7 2.1 pad_maximum_fusion.3
  59.8 29.1 %all-to-all-start.1 = ((bf16[4,64,2176]{2,0,1:T(4,128)(2,1)}), bf16[4,64,2176]{2,0,1:T(4,128)(2,1)S(1)}, u32[]{:S(2)}, u32[]{:S(2)}) async-start(bf16[4,64,2176]{2,0,1:T(4,128)(2,1)} %pad_maximum_fusion.3), calls=%async_computation.1 | async-start | bytes 2228224 | tf_op jit(solution)/shard_map/all_to_all | solution.py:71
  89.0 4.5 %reshape.104 = bf16[64,2,64,2]{3,2,1,0:T(8,128)(2,1)S(1)} reshape(bf16[128,128]{1,0:T(8,128)(2,1)S(1)} %copy-done.5) | data formatting | bytes 65536 | tf_op jit(solution)/shard_map/reshape | solution.py:75
  93.6 1.1 copy.399
  94.7 4.5 %reshape.106 = bf16[64,2,64,2]{3,2,1,0:T(8,128)(2,1)S(1)} reshape(bf16[128,128]{1,0:T(8,128)(2,1)S(1)} %copy-done.6) | data formatting | bytes 65536 | tf_op jit(solution)/shard_map/reshape | solution.py:75
  99.3 1.1 copy.400
  100.5 103.8 %all-to-all-done.1 = bf16[4,64,2176]{2,0,1:T(4,128)(2,1)S(1)} async-done(((bf16[4,64,2176]{2,0,1:T(4,128)(2,1)}), bf16[4,64,2176]{2,0,1:T(4,128)(2,1)S(1)}, u32[]{:S(2)}, u32[]{:S(2)}) %all-to-all-start.1) | async-done | bytes 1114144 | tf_op jit(solution)/shard_map/all_to_all | solution.py:71
  204.3 0.8 fusion.33
  205.2 0.8 fusion.12
  206.1 0.8 fusion.3
  206.9 0.8 select_reduce_fusion.1
  207.7 0.9 fusion.2
  208.7 1.9 copy.402
  210.6 5.5 %all-to-all-start.2 = ((bf16[4,64,2176]{2,0,1:T(4,128)(2,1)}), bf16[4,64,2176]{2,0,1:T(4,128)(2,1)S(1)}, u32[]{:S(2)}, u32[]{:S(2)}) async-start(bf16[4,64,2176]{2,0,1:T(4,128)(2,1)} %copy.402), calls=%async_computation.2 | async-start | bytes 2228224 | tf_op jit(solution)/shard_map/all_to_all | solution.py:114
  216.1 115.4 %all-to-all-done.2 = bf16[4,64,2176]{2,0,1:T(4,128)(2,1)S(1)} async-done(((bf16[4,64,2176]{2,0,1:T(4,128)(2,1)}), bf16[4,64,2176]{2,0,1:T(4,128)(2,1)S(1)}, u32[]{:S(2)}, u32[]{:S(2)}) %all-to-all-start.2) | async-done | bytes 1114144 | tf_op jit(solution)/shard_map/all_to_all | solution.py:114
  331.5 0.8 fusion.32
  333.0 0.9 copy-done.3
  334.0 0.5 fusion.10
  334.5 0.5 fusion.6
  335.2 1.0 copy-done.1
  336.2 0.5 fusion.9
  336.7 0.5 fusion.7
  337.2 0.2 pad_maximum_fusion.2
  337.4 0.6 copy.522
  338.0 2.8 copy.442
  341.1 1.8 pad_maximum_fusion.1
  342.9 2.1 gather_fusion.1
  344.9 1.9 broadcast_select_fusion
  346.8 32.7 %all_to_all.20 = bf16[16,136,512]{2,1,0:T(8,128)(2,1)S(1)} all-to-all(bf16[16,136,512]{2,1,0:T(8,128)(2,1)S(1)} %broadcast_select_fusion), channel_id=1, replica_groups=mesh['seq'=16,'row'=8,'col'=8] {'seq'}, dimensions={0} | all-to-all | bytes 4456448 | tf_op jit(solution)/shard_map/all_to_all | solution.py:130
  379.6 0.7 fusion.35
  380.2 0.3 slice_reduce_fusion
  380.5 0.7 fusion.34
  (177 shorter events, 3.7 us)
Async XLA Ops:
  4.1 7.2 %copy-start.7 = (s32[16]{0:T(128)S(1)}, s32[16]{0:T(128)}, u32[]{:S(2)}) copy-start(s32[16]{0:T(128)} %param.15) | copy-start | bytes 196
  4.1 39.2 %all-to-all-start = ((bf16[16,136,512]{2,1,0:T(8,128)(2,1)}), bf16[16,136,512]{2,1,0:T(8,128)(2,1)S(1)}, u32[]{:S(2)}, u32[]{:S(2)}) async-start(bf16[16,136,512]{2,1,0:T(8,128)(2,1)} %pad_maximum_fusion), calls=%async_computation | async-start | bytes 4456448 | tf_op jit(solution)/shard_map/all_to_all | solution.py:32
  53.1 1.0 copy-start.2
  53.1 1.3 copy-start
  53.5 1.3 copy-start.4
  54.9 0.8 slice-start
  59.8 29.2 %copy-start.5 = (bf16[128,128]{1,0:T(8,128)(2,1)S(1)}, bf16[128,128]{1,0:T(8,128)(2,1)}, u32[]{:S(2)}) copy-start(bf16[128,128]{1,0:T(8,128)(2,1)} %param.13) | copy-start | bytes 98308
  59.8 144.5 %all-to-all-start.1 = ((bf16[4,64,2176]{2,0,1:T(4,128)(2,1)}), bf16[4,64,2176]{2,0,1:T(4,128)(2,1)S(1)}, u32[]{:S(2)}, u32[]{:S(2)}) async-start(bf16[4,64,2176]{2,0,1:T(4,128)(2,1)} %pad_maximum_fusion.3), calls=%async_computation.1 | async-start | bytes 2228224 | tf_op jit(solution)/shard_map/all_to_all | solution.py:71
  93.5 1.2 copy-start.6
  210.6 121.0 %all-to-all-start.2 = ((bf16[4,64,2176]{2,0,1:T(4,128)(2,1)}), bf16[4,64,2176]{2,0,1:T(4,128)(2,1)S(1)}, u32[]{:S(2)}, u32[]{:S(2)}) async-start(bf16[4,64,2176]{2,0,1:T(4,128)(2,1)} %copy.402), calls=%async_computation.2 | async-start | bytes 2228224 | tf_op jit(solution)/shard_map/all_to_all | solution.py:114
  332.7 1.2 copy-start.3
  335.0 1.2 copy-start.1

commit v2 on v1

v2 whole, which is shorter than its diff:
```python
import functools

import jax
import jax.numpy as jnp
from jax import lax
from jax.experimental import pallas as pl
from jax.experimental.pallas import tpu as pltpu
from jax.sharding import PartitionSpec as P

DH = 128


logit_cap = 10.0

HEAD_AXES = ("row", "col")
KINDS = 4
CHUNK = 4
INTERP = False


def place_of(p, b, half, blocks, rows):
    return (b if p < half else blocks - p + b) * rows


def pair_of(p, half, blocks):
    return p if p < half else blocks - 1 - p


def send_kernel(query_ref, key_ref, value_ref, grad_ref, out_ref, *, blocks, rows, strip, width):
    for s in range(blocks):
        out_ref[s, :rows, :width] = key_ref[...]
        out_ref[s, :rows, width:] = value_ref[...]
        out_ref[s, rows:, :width] = query_ref[s * strip : (s + 1) * strip, :]
        out_ref[s, rows:, width:] = grad_ref[s * strip : (s + 1) * strip, :]


def score_kernel(
    order_ref, received_ref, out_ref, key_value_ref, spread_ref, lines_ref, *, blocks, rows, strip, scaling
):
    half = blocks // 2
    group = KINDS * strip
    for p in range(blocks):
        source = order_ref[p]
        key_value_ref[p * rows : (p + 1) * rows, :] = received_ref[source, :rows, :]
        lines_ref[p * strip : (p + 1) * strip, :] = received_ref[source, rows:, :].astype(jnp.float32)
    total = blocks * group
    row = lax.broadcasted_iota(jnp.int32, (total, blocks * strip), 0)
    line = lax.broadcasted_iota(jnp.int32, (total, blocks * strip), 1)
    repeat = jnp.where(row // KINDS == line, 1.0, 0.0).astype(jnp.bfloat16)
    repeated = jnp.dot(
        repeat, lines_ref[...].astype(jnp.bfloat16), preferred_element_type=jnp.float32
    )
    row = lax.broadcasted_iota(jnp.int32, (total, KINDS * DH), 0)
    column = lax.broadcasted_iota(jnp.int32, (total, KINDS * DH), 1)
    spread_ref[...] = jnp.where(row % KINDS == column // DH, repeated, 0.0).astype(jnp.bfloat16)
    for j in range(blocks // CHUNK):
        first = j * CHUNK
        keys = key_value_ref[first * rows : (first + CHUNK) * rows, :]
        scores = lax.dot_general(
            spread_ref[first * group :, :],
            keys,
            (((1,), (1,)), ((), ())),
            preferred_element_type=jnp.float32,
        )
        kind = lax.broadcasted_iota(jnp.int32, scores.shape, 0) % KINDS
        scores = jnp.where(kind < KINDS // 2, scores * scaling, scores).astype(jnp.bfloat16)
        for p in range(first, blocks):
            count = min(p - first + 1, CHUNK)
            c = pair_of(p, half, blocks)
            lane = place_of(p, first, half, blocks, rows)
            out_ref[c * group : (c + 1) * group, lane : lane + count * rows] = scores[
                (p - first) * group : (p - first + 1) * group, : count * rows
            ]


def mix_kernel(
    where_ref, incoming_ref, before_ref, after_ref, out_ref, squashed_ref, weight_ref, grad_ref, both_ref,
    *, blocks, rows, heads, scaling
):
    pair, offset = where_ref[0], where_ref[1]
    zero = jnp.zeros((heads, rows), jnp.float32)
    near_total, far_total, near_dot, far_dot = zero, zero, zero, zero
    lane = lax.broadcasted_iota(jnp.int32, (heads, rows), 1)
    tiles = blocks + 1
    for j in range(tiles):
        cut = slice(j * rows, (j + 1) * rows)
        mixed = jnp.dot(
            before_ref[...], incoming_ref[:, cut], preferred_element_type=jnp.float32
        )
        is_near = j <= pair
        start = (j - jnp.where(is_near, 0, pair + 1)) * rows
        limit = jnp.where(is_near, pair, blocks - 1 - pair) * rows + offset - start
        squashed = jnp.tanh(mixed[:heads] / logit_cap)
        weights = jnp.where(lane <= limit, jnp.exp(logit_cap * squashed), 0.0)
        grad_probs = mixed[heads:]
        squashed_ref[:, cut] = squashed
        weight_ref[:, cut] = weights
        grad_ref[:, cut] = grad_probs
        dots = weights * grad_probs
        near = jnp.where(is_near, 1.0, 0.0)
        near_total += weights * near
        far_total += weights * (1.0 - near)
        near_dot += dots * near
        far_dot += dots * (1.0 - near)

    def down(values):
        return jnp.sum(values, axis=1, keepdims=True)

    near_scale, far_scale = 1.0 / down(near_total), 1.0 / down(far_total)
    near_row, far_row = down(near_dot) * near_scale, down(far_dot) * far_scale
    for j in range(tiles):
        cut = slice(j * rows, (j + 1) * rows)
        is_near = j <= pair
        probs = weight_ref[:, cut] * jnp.where(is_near, near_scale, far_scale)
        squashed = squashed_ref[:, cut]
        grad_capped = probs * (grad_ref[:, cut] - jnp.where(is_near, near_row, far_row))
        both_ref[:heads, cut] = (grad_capped * (1.0 - squashed * squashed)).astype(jnp.bfloat16)
        both_ref[heads:, cut] = probs.astype(jnp.bfloat16)
        result = jnp.dot(after_ref[...], both_ref[:, cut], preferred_element_type=jnp.float32)
        kind = lax.broadcasted_iota(jnp.int32, result.shape, 0) % KINDS
        out_ref[:, cut] = jnp.where(kind < KINDS // 2, result * scaling, result).astype(jnp.bfloat16)


def grad_kernel(
    order_ref, incoming_ref, key_value_ref, spread_ref, out_ref, dense_ref, sum_ref, *, blocks, rows, strip
):
    half = blocks // 2
    group = KINDS * strip
    for p in range(blocks):
        c = pair_of(p, half, blocks)
        lane = place_of(p, 0, half, blocks, rows)
        count = (p + 1) * rows
        padded = (p // CHUNK + 1) * CHUNK * rows
        dense_ref[p * group : (p + 1) * group, :count] = incoming_ref[
            c * group : (c + 1) * group, lane : lane + count
        ]
        if padded > count:
            dense_ref[p * group : (p + 1) * group, count:padded] = jnp.zeros(
                (group, padded - count), jnp.bfloat16
            )
    for j in range(blocks // CHUNK):
        first = j * CHUNK
        cut = slice(first * rows, (first + CHUNK) * rows)
        dense = dense_ref[first * group :, cut]
        terms = lax.dot_general(
            dense,
            spread_ref[first * group :, :],
            (((0,), (0,)), ((), ())),
            preferred_element_type=jnp.float32,
        ).astype(jnp.bfloat16)
        for b in range(CHUNK):
            out_ref[order_ref[first + b], :rows, :] = terms[b * rows : (b + 1) * rows, :]
        added = jnp.dot(dense, key_value_ref[cut, :], preferred_element_type=jnp.float32)
        for kind in range(KINDS):
            columns = slice(kind * DH, (kind + 1) * DH)
            if j == 0:
                sum_ref[kind] = added[:, columns]
            else:
                sum_ref[kind, first * group : blocks * group, :] += added[:, columns]
    for kind in range(KINDS):
        columns = slice(kind * DH, (kind + 1) * DH)
        lines = sum_ref.at[kind][pl.ds(kind, blocks * strip, stride=KINDS), :].astype(jnp.bfloat16)
        for p in range(blocks):
            out_ref[order_ref[p], rows:, columns] = lines[p * strip : (p + 1) * strip, :]


def body(query_rows, key_rows, value_rows, out_grad, mix_pre, mix_post, block_order):
    blocks = lax.axis_size("seq")
    owners = lax.axis_size("row") * lax.axis_size("col")
    rows, width = query_rows.shape
    heads_local = width // DH
    heads = mix_pre.shape[0]
    scaling = DH ** (-0.5)
    strip = rows // blocks
    half = blocks // 2
    span = (blocks + 1) * rows
    seq_len = blocks * rows
    packed_rows = owners * KINDS
    spread_rows = rows * KINDS
    bf16, f32 = jnp.bfloat16, jnp.float32
    whole = pl.BlockSpec(memory_space=pltpu.VMEM)
    table = pl.BlockSpec(memory_space=pltpu.SMEM)
    exchange_shape = (blocks, rows + strip, 2 * width)

    def call(kernel, ins, outs, scratch=(), **static):
        return pl.pallas_call(
            functools.partial(kernel, **static),
            in_specs=ins,
            out_specs=[whole] * len(outs),
            out_shape=[jax.ShapeDtypeStruct(shape, bf16) for shape in outs],
            scratch_shapes=scratch,
            interpret=INTERP,
        )

    (sent,) = call(
        send_kernel, [whole] * 4, [exchange_shape], blocks=blocks, rows=rows, strip=strip, width=width
    )(query_rows, key_rows, value_rows, out_grad)
    received = lax.all_to_all(sent, "seq", split_axis=0, concat_axis=0, tiled=True)
    numbers = jnp.arange(blocks, dtype=jnp.int32)
    stored_at = jnp.sum(
        jnp.where(block_order[None, :] == numbers[:, None], numbers[None, :], 0), axis=1
    )

    packed, key_value, spread = call(
        score_kernel,
        [table, whole],
        [(packed_rows, span), (seq_len, 2 * width), (spread_rows, 2 * width)],
        [pltpu.VMEM((rows, 2 * width), f32)],
        blocks=blocks, rows=rows, strip=strip, scaling=scaling,
    )(stored_at, received)

    def exchange(values):
        return lax.all_to_all(
            values.reshape(owners, KINDS, span), HEAD_AXES, split_axis=0, concat_axis=0, tiled=True
        ).reshape(packed_rows, span)

    empty = jnp.zeros((heads, owners, heads_local), bf16)
    into_scores = jnp.concatenate([mix_pre.reshape(heads, owners, heads_local), empty], axis=2)
    into_grads = jnp.concatenate([empty, mix_post.T.reshape(heads, owners, heads_local)], axis=2)
    before = jnp.concatenate([into_scores, into_grads], axis=0).reshape(2 * heads, packed_rows)
    out_scores = mix_pre.T.reshape(owners, heads_local, heads)
    out_probs = mix_post.reshape(owners, heads_local, heads)
    blank = jnp.zeros((owners, heads_local, heads), bf16)
    after = jnp.concatenate(
        [
            jnp.concatenate([out_scores, blank], axis=1),
            jnp.concatenate([blank, out_probs], axis=1),
        ],
        axis=2,
    ).reshape(packed_rows, 2 * heads)
    own = lax.axis_index(HEAD_AXES)
    where = jnp.stack([own // strip, lax.axis_index("seq") * strip + own % strip]).astype(jnp.int32)
    (mixed,) = call(
        mix_kernel,
        [table, whole, whole, whole],
        [(packed_rows, span)],
        [
            pltpu.VMEM((heads, span), f32),
            pltpu.VMEM((heads, span), f32),
            pltpu.VMEM((heads, span), f32),
            pltpu.VMEM((2 * heads, span), bf16),
        ],
        blocks=blocks, rows=rows, heads=heads, scaling=scaling,
    )(where, exchange(packed), before, after)

    (sent,) = call(
        grad_kernel,
        [table, whole, whole, whole],
        [exchange_shape],
        [pltpu.VMEM((spread_rows, seq_len), bf16), pltpu.VMEM((KINDS, spread_rows, DH), f32)],
        blocks=blocks, rows=rows, strip=strip,
    )(stored_at, exchange(mixed), key_value, spread)
    received = lax.all_to_all(sent, "seq", split_axis=0, concat_axis=0, tiled=True)
    summed = jnp.sum(received[:, :rows].astype(f32), axis=0).astype(bf16)
    lines = received[:, rows:].reshape(rows, 2 * width)
    return (lines[:, width:], lines[:, :width], summed[:, :width], summed[:, width:])


def solution(mesh):
    spread = P("seq", HEAD_AXES)
    return jax.shard_map(
        body,
        mesh=mesh,
        in_specs=(spread, spread, spread, spread, P(), P(), P()),
        out_specs=(spread, spread, spread, spread),
        check_vma=False,
    )
```

time: 382 us -> 363 us (0.950)
  blocking collectives: 32.7 us -> 154 us
  waiting for transfers between devices: 251 us -> 144 us
  local copies, waits for them, and re-layouts: 34.2 us -> 9.49 us
  Pallas kernels: 0 us -> 16.2 us
  other arithmetic: 12.9 us -> 1.67 us
  matrix products: 6.26 us -> 0 us
  starting transfers between devices: 41.8 us -> 36.2 us
    all_to_all x0 -> x1, blocking collectives: none -> 120 us  [exchange(): lax.all_to_all(values.reshape(owners, KINDS, span), HEAD_AXES, split_axis...]
    all_to_all x2 -> x1, waiting for transfers between devices: 219 us -> 113 us  [exchange(): lax.all_to_all(values.reshape(owners, KINDS, span), HEAD_AXES, split_axis...]
    pallas_call x0 -> x4, Pallas kernels: none -> 16.2 us  [the longest x1 5.14 us: body(): call(grad_kernel, [table, whole, whole, whole], [exchange_shape], [pltpu....]
    reshape x10 -> x8, local copies, waits for them, and re-layouts: 16.6 us -> 7.3 us  [the longest x2 3.55 us: exchange(): values.reshape(owners, KINDS, span)]
    concatenate x6 -> x2, other arithmetic: 6.56 us -> 0.17 us  [the longest x1 0.09 us: body(): jnp.concatenate([into_scores, into_grads], axis=0)]
    dot_general x10 -> x0, matrix products: 6.26 us -> none  [the longest x4 2.02 us: rounded(): jnp.einsum(spec, left, right, preferred_element_type=jnp.float32)]
    slice x40 -> x0, local copies, waits for them, and re-layouts: 5.66 us -> none  [the longest x1 1.55 us: body(): key_value_all = by_place[:, :rows].reshape(seq_len, 2, heads_local, DH)]
    all_to_all x2 -> x1, starting transfers between devices: 34.6 us -> 29 us  [exchange(): lax.all_to_all(values.reshape(owners, KINDS, span), HEAD_AXES, split_axis...]
  transfers between devices with their start and end apart: 3 -> 2, of which waited for: 3 -> 2; matrix products, arithmetic and copies ran while one was open for 3% -> 1% of each run, Pallas kernels for 0% -> 0%
where the time goes in v2:
time: 363 us; the launch traced here: 362 us
  blocking collectives  154 us (42%)
  waiting for transfers between devices  144 us (40%)
  starting transfers between devices  36.2 us (10%)
  Pallas kernels  16.2 us (4%)
  local copies, waits for them, and re-layouts  9.49 us (3%)
    all_to_all x1, blocking collectives, exchange(): lax.all_to_all(values.reshape(owners, KINDS, span), HEAD_AXES, split_axis...  120 us
    all_to_all x1, waiting for transfers between devices, exchange(): lax.all_to_all(values.reshape(owners, KINDS, span), HEAD_AXES, split_axis...  113 us
    all_to_all x1, blocking collectives, body(): lax.all_to_all(sent, 'seq', split_axis=0, concat_axis=0, tiled=True)  33.7 us
    all_to_all x1, waiting for transfers between devices, body(): lax.all_to_all(sent, 'seq', split_axis=0, concat_axis=0, tiled=True)  31.4 us
    all_to_all x1, starting transfers between devices, exchange(): lax.all_to_all(values.reshape(owners, KINDS, span), HEAD_AXES, split_axis...  29 us
  transfers between devices with their start and end apart: 2, of which 2 were waited for; matrix products, arithmetic and copies ran while one was open for 1% of the time, Pallas kernels for 0%

profile of v2, /device:TPU:32, one launch (start us, length us, event | category | flops | bytes accessed | tf_op | source)
XLA Modules:
  0.0 362.4 jit_solution(15548036551615635851)
XLA Ops:
  0.6 2.5 shard_map.102
  3.1 0.0 copy-start.3
  3.1 7.2 %all-to-all-start = ((bf16[16,136,512]{2,1,0:T(8,128)(2,1)}), bf16[16,136,512]{2,1,0:T(8,128)(2,1)S(1)}, u32[]{:S(2)}, u32[]{:S(2)}) async-start(bf16[16,136,512]{2,1,0:T(8,128)(2,1)} %shard_map.102), calls=%async_computation | async-start | bytes 4456448 | tf_op jit(solution)/shard_map/all_to_all | solution.py:198
  10.3 0.0 copy-done.3
  10.3 0.6 select_reduce_fusion.order_ref
  10.9 31.4 %all-to-all-done.received_ref = bf16[16,136,512]{2,1,0:T(8,128)(2,1)S(1)} async-done(((bf16[16,136,512]{2,1,0:T(8,128)(2,1)}), bf16[16,136,512]{2,1,0:T(8,128)(2,1)S(1)}, u32[]{:S(2)}, u32[]{:S(2)}) %all-to-all-start) | async-done | bytes 2228256 | tf_op jit(solution)/shard_map/all_to_all | solution.py:198
  42.3 0.0 copy-start
  42.3 1.4 copy-done
  43.7 4.3 %shard_map.103 = (bf16[256,2176]{1,0:T(8,128)(2,1)}, bf16[2048,512]{1,0:T(8,128)(2,1)}, bf16[512,512]{1,0:T(8,128)(2,1)}) custom-call(s32[16]{0:T(128)} %select_reduce_fusion.order_ref, bf16[16,136,512]{2,1,0:T(8,128)(2,1)} %copy-done), custom_call_target="tpu_custom_call" | custom-call | tf_op jit(solution)/shard_map/pallas_call | solution.py:204
  48.0 0.0 copy-start.2
  48.0 0.0 copy-start.1
  48.0 2.2 reshape.42
  50.2 29.0 %all-to-all-start.1 = ((bf16[64,4,2176]{2,1,0:T(4,128)(2,1)}), bf16[64,4,2176]{2,1,0:T(4,128)(2,1)S(1)}, u32[]{:S(2)}, u32[]{:S(2)}) async-start(bf16[64,4,2176]{2,1,0:T(4,128)(2,1)} %reshape.42), calls=%async_computation.1 | async-start | bytes 2228224 | tf_op jit(solution)/shard_map/all_to_all | solution.py:213
  79.2 0.0 copy-done.2
  79.3 0.1 copy.16
  79.4 0.0 copy-done.1
  79.4 0.1 fusion.5
  79.5 0.8 copy.18.before_ref
  80.3 0.1 fusion.4
  80.4 0.7 reshape.49.after_ref
  81.1 0.6 pad_add_fusion.where_ref
  81.6 112.9 %all-to-all-done.1 = bf16[64,4,2176]{2,1,0:T(4,128)(2,1)S(1)} async-done(((bf16[64,4,2176]{2,1,0:T(4,128)(2,1)}), bf16[64,4,2176]{2,1,0:T(4,128)(2,1)S(1)}, u32[]{:S(2)}, u32[]{:S(2)}) %all-to-all-start.1) | async-done | bytes 1114144 | tf_op jit(solution)/shard_map/all_to_all | solution.py:213
  194.6 1.1 reshape.43.incoming_ref
  195.7 4.3 %shard_map.104 = bf16[256,2176]{1,0:T(8,128)(2,1)} custom-call(s32[2]{0:T(128)} %pad_add_fusion.where_ref, bf16[256,2176]{1,0:T(8,128)(2,1)} %reshape.43.incoming_ref, bf16[256,256]{1,0:T(8,128)(2,1)} %copy.18.before_ref, bf16[256,256]{1,0:T(8,128)(2,1)} %reshape.49.after_ref), custom_call_target="tpu_custom_call" | custom-call | tf_op jit(solution)/shard_map/pallas_call | solution.py:233
  200.0 1.4 reshape.50
  201.4 120.1 %all_to_all.20 = bf16[64,4,2176]{2,1,0:T(4,128)(2,1)S(1)} all-to-all(bf16[64,4,2176]{2,1,0:T(4,128)(2,1)S(1)} %reshape.50), channel_id=1, replica_groups=mesh['seq'=16,'row'=8,'col'=8] {'row','col'}, dimensions={0} | all-to-all | bytes 2228224 | tf_op jit(solution)/shard_map/all_to_all | solution.py:213
  321.5 1.1 reshape.51.incoming_ref
  322.6 5.1 %shard_map.105 = bf16[16,136,512]{2,1,0:T(8,128)(2,1)} custom-call(s32[16]{0:T(128)} %select_reduce_fusion.order_ref, bf16[256,2176]{1,0:T(8,128)(2,1)} %reshape.51.incoming_ref, bf16[2048,512]{1,0:T(8,128)(2,1)} %get-tuple-element.8.key_value_ref, bf16[512,512]{1,0:T(8,128)(2,1)} %get-tuple-element.9.spread_ref), custom_call_target="tpu_custom_call" | custom-call | tf_op jit(solution)/shard_map/pallas_call | solution.py:246
  327.8 33.7 %all_to_all.21 = bf16[16,136,512]{2,1,0:T(8,128)(2,1)S(1)} all-to-all(bf16[16,136,512]{2,1,0:T(8,128)(2,1)} %shard_map.105), channel_id=1, replica_groups=mesh['seq'=16,'row'=8,'col'=8] {'seq'}, dimensions={0} | all-to-all | bytes 4456448 | tf_op jit(solution)/shard_map/all_to_all | solution.py:253
  361.4 0.3 slice_reduce_fusion
  361.7 0.7 fusion.6
  (2 shorter events, 0.0 us)
Async XLA Ops:
  3.1 7.2 %copy-start.3 = (s32[16]{0:T(128)S(1)}, s32[16]{0:T(128)}, u32[]{:S(2)}) copy-start(s32[16]{0:T(128)} %param.13) | copy-start | bytes 196
  3.1 39.2 %all-to-all-start = ((bf16[16,136,512]{2,1,0:T(8,128)(2,1)}), bf16[16,136,512]{2,1,0:T(8,128)(2,1)S(1)}, u32[]{:S(2)}, u32[]{:S(2)}) async-start(bf16[16,136,512]{2,1,0:T(8,128)(2,1)} %shard_map.102), calls=%async_computation | async-start | bytes 4456448 | tf_op jit(solution)/shard_map/all_to_all | solution.py:198
  42.3 1.4 copy-start
  48.0 31.2 %copy-start.2 = (bf16[128,128]{1,0:T(8,128)(2,1)S(1)}, bf16[128,128]{1,0:T(8,128)(2,1)}, u32[]{:S(2)}) copy-start(bf16[128,128]{1,0:T(8,128)(2,1)} %param.11) | copy-start | bytes 98308
  48.0 31.3 %copy-start.1 = (bf16[128,128]{1,0:T(8,128)(2,1)S(1)}, bf16[128,128]{1,0:T(8,128)(2,1)}, u32[]{:S(2)}) copy-start(bf16[128,128]{1,0:T(8,128)(2,1)} %param.12) | copy-start | bytes 98308
  50.2 144.4 %all-to-all-start.1 = ((bf16[64,4,2176]{2,1,0:T(4,128)(2,1)}), bf16[64,4,2176]{2,1,0:T(4,128)(2,1)S(1)}, u32[]{:S(2)}, u32[]{:S(2)}) async-start(bf16[64,4,2176]{2,1,0:T(4,128)(2,1)} %reshape.42), calls=%async_computation.1 | async-start | bytes 2228224 | tf_op jit(solution)/shard_map/all_to_all | solution.py:213

commit v3 on v2

--- a/solution.py
+++ b/solution.py
@@ -15,6 +15,7 @@
 HEAD_AXES = ("row", "col")
 KINDS = 4
 CHUNK = 4
+VMEM_LIMIT = 24 << 20
 INTERP = False
 
 
@@ -34,11 +35,12 @@
         out_ref[s, rows:, width:] = grad_ref[s * strip : (s + 1) * strip, :]
 
 
-def score_kernel(
-    order_ref, received_ref, out_ref, key_value_ref, spread_ref, lines_ref, *, blocks, rows, strip, scaling
+def sort_blocks(
+    block_ref, received_ref, order_ref, key_value_ref, spread_ref, lines_ref, blocks, rows, strip
 ):
-    half = blocks // 2
     group = KINDS * strip
+    for s in range(blocks):
+        order_ref[block_ref[s]] = s
     for p in range(blocks):
         source = order_ref[p]
         key_value_ref[p * rows : (p + 1) * rows, :] = received_ref[source, :rows, :]
@@ -53,6 +55,17 @@
     row = lax.broadcasted_iota(jnp.int32, (total, KINDS * DH), 0)
     column = lax.broadcasted_iota(jnp.int32, (total, KINDS * DH), 1)
     spread_ref[...] = jnp.where(row % KINDS == column // DH, repeated, 0.0).astype(jnp.bfloat16)
+
+
+def score_kernel(
+    block_ref, received_ref, out_ref, order_ref, key_value_ref, spread_ref, lines_ref,
+    *, blocks, rows, strip, scaling
+):
+    half = blocks // 2
+    group = KINDS * strip
+    sort_blocks(
+        block_ref, received_ref, order_ref, key_value_ref, spread_ref, lines_ref, blocks, rows, strip
+    )
     for j in range(blocks // CHUNK):
         first = j * CHUNK
         keys = key_value_ref[first * rows : (first + CHUNK) * rows, :]
@@ -68,16 +81,39 @@
             count = min(p - first + 1, CHUNK)
             c = pair_of(p, half, blocks)
             lane = place_of(p, first, half, blocks, rows)
-            out_ref[c * group : (c + 1) * group, lane : lane + count * rows] = scores[
+            out_ref[c * strip : (c + 1) * strip, :, lane : lane + count * rows] = scores[
                 (p - first) * group : (p - first + 1) * group, : count * rows
-            ]
+            ].reshape(strip, KINDS, count * rows)
 
 
 def mix_kernel(
-    where_ref, incoming_ref, before_ref, after_ref, out_ref, squashed_ref, weight_ref, grad_ref, both_ref,
-    *, blocks, rows, heads, scaling
+    incoming_ref, pre_ref, post_ref, out_ref, before_ref, after_ref, squashed_ref, weight_ref, grad_ref,
+    both_ref, *, blocks, rows, strip, heads, scaling
 ):
-    pair, offset = where_ref[0], where_ref[1]
+    own = lax.axis_index(HEAD_AXES)
+    pair = lax.div(own, strip)
+    offset = lax.axis_index("seq") * strip + lax.rem(own, strip)
+    shape = (heads, before_ref.shape[1])
+    row = lax.broadcasted_iota(jnp.int32, shape, 0)
+    column = lax.broadcasted_iota(jnp.int32, shape, 1)
+    kind = column % KINDS
+    here = column // KINDS * (KINDS // 2) + kind % (KINDS // 2) == row
+    pick_scores = jnp.where(here & (kind < KINDS // 2), 1.0, 0.0).astype(jnp.bfloat16)
+    pick_probs = jnp.where(here & (kind >= KINDS // 2), 1.0, 0.0).astype(jnp.bfloat16)
+
+    def pick(left, right, left_dim, right_dim):
+        return lax.dot_general(
+            left,
+            right,
+            (((left_dim,), (right_dim,)), ((), ())),
+            preferred_element_type=jnp.float32,
+        ).astype(jnp.bfloat16)
+
+    pre, post = pre_ref[...], post_ref[...]
+    before_ref[:heads, :] = pick(pre, pick_scores, 1, 0)
+    before_ref[heads:, :] = pick(post, pick_probs, 0, 0)
+    after_ref[:, :heads] = pick(pick_scores, pre, 0, 1)
+    after_ref[:, heads:] = pick(pick_probs, post, 0, 0)
     zero = jnp.zeros((heads, rows), jnp.float32)
     near_total, far_total, near_dot, far_dot = zero, zero, zero, zero
     lane = lax.broadcasted_iota(jnp.int32, (heads, rows), 1)
@@ -85,7 +121,7 @@
     for j in range(tiles):
         cut = slice(j * rows, (j + 1) * rows)
         mixed = jnp.dot(
-            before_ref[...], incoming_ref[:, cut], preferred_element_type=jnp.float32
+            before_ref[...], incoming_ref[:, :, cut].reshape(before_ref.shape[1], rows), preferred_element_type=jnp.float32
         )
         is_near = j <= pair
         start = (j - jnp.where(is_near, 0, pair + 1)) * rows
@@ -118,22 +154,27 @@
         both_ref[heads:, cut] = probs.astype(jnp.bfloat16)
         result = jnp.dot(after_ref[...], both_ref[:, cut], preferred_element_type=jnp.float32)
         kind = lax.broadcasted_iota(jnp.int32, result.shape, 0) % KINDS
-        out_ref[:, cut] = jnp.where(kind < KINDS // 2, result * scaling, result).astype(jnp.bfloat16)
+        out_ref[:, :, cut] = jnp.where(kind < KINDS // 2, result * scaling, result).astype(jnp.bfloat16).reshape(out_ref.shape[0], KINDS, rows)
 
 
 def grad_kernel(
-    order_ref, incoming_ref, key_value_ref, spread_ref, out_ref, dense_ref, sum_ref, *, blocks, rows, strip
+    block_ref, incoming_ref, received_ref, out_ref, dense_ref, sum_ref, order_ref, key_value_ref,
+    spread_ref, lines_ref,
+    *, blocks, rows, strip
 ):
     half = blocks // 2
     group = KINDS * strip
+    sort_blocks(
+        block_ref, received_ref, order_ref, key_value_ref, spread_ref, lines_ref, blocks, rows, strip
+    )
     for p in range(blocks):
         c = pair_of(p, half, blocks)
         lane = place_of(p, 0, half, blocks, rows)
         count = (p + 1) * rows
         padded = (p // CHUNK + 1) * CHUNK * rows
         dense_ref[p * group : (p + 1) * group, :count] = incoming_ref[
-            c * group : (c + 1) * group, lane : lane + count
-        ]
+            c * strip : (c + 1) * strip, :, lane : lane + count
+        ].reshape(group, count)
         if padded > count:
             dense_ref[p * group : (p + 1) * group, count:padded] = jnp.zeros(
                 (group, padded - count), jnp.bfloat16
@@ -189,67 +230,60 @@
             out_specs=[whole] * len(outs),
             out_shape=[jax.ShapeDtypeStruct(shape, bf16) for shape in outs],
             scratch_shapes=scratch,
+            compiler_params=pltpu.CompilerParams(vmem_limit_bytes=VMEM_LIMIT),
             interpret=INTERP,
         )
+
+    def near(values):
+        if INTERP:
+            return values
+        return pltpu.with_memory_space_constraint(values, pltpu.VMEM)
 
     (sent,) = call(
         send_kernel, [whole] * 4, [exchange_shape], blocks=blocks, rows=rows, strip=strip, width=width
     )(query_rows, key_rows, value_rows, out_grad)
-    received = lax.all_to_all(sent, "seq", split_axis=0, concat_axis=0, tiled=True)
-    numbers = jnp.arange(blocks, dtype=jnp.int32)
-    stored_at = jnp.sum(
-        jnp.where(block_order[None, :] == numbers[:, None], numbers[None, :], 0), axis=1
-    )
-
-    packed, key_value, spread = call(
+    received = near(lax.all_to_all(sent, "seq", split_axis=0, concat_axis=0, tiled=True))
+
+    sorted_blocks = [
+        pltpu.SMEM((blocks,), jnp.int32),
+        pltpu.VMEM((seq_len, 2 * width), bf16),
+        pltpu.VMEM((spread_rows, 2 * width), bf16),
+        pltpu.VMEM((rows, 2 * width), f32),
+    ]
+    (packed,) = call(
         score_kernel,
         [table, whole],
-        [(packed_rows, span), (seq_len, 2 * width), (spread_rows, 2 * width)],
-        [pltpu.VMEM((rows, 2 * width), f32)],
+        [(owners, KINDS, span)],
+        sorted_blocks,
         blocks=blocks, rows=rows, strip=strip, scaling=scaling,
-    )(stored_at, received)
+    )(block_order, received)
 
     def exchange(values):
-        return lax.all_to_all(
-            values.reshape(owners, KINDS, span), HEAD_AXES, split_axis=0, concat_axis=0, tiled=True
-        ).reshape(packed_rows, span)
-
-    empty = jnp.zeros((heads, owners, heads_local), bf16)
-    into_scores = jnp.concatenate([mix_pre.reshape(heads, owners, heads_local), empty], axis=2)
-    into_grads = jnp.concatenate([empty, mix_post.T.reshape(heads, owners, heads_local)], axis=2)
-    before = jnp.concatenate([into_scores, into_grads], axis=0).reshape(2 * heads, packed_rows)
-    out_scores = mix_pre.T.reshape(owners, heads_local, heads)
-    out_probs = mix_post.reshape(owners, heads_local, heads)
-    blank = jnp.zeros((owners, heads_local, heads), bf16)
-    after = jnp.concatenate(
-        [
-            jnp.concatenate([out_scores, blank], axis=1),
-            jnp.concatenate([blank, out_probs], axis=1),
-        ],
-        axis=2,
-    ).reshape(packed_rows, 2 * heads)
-    own = lax.axis_index(HEAD_AXES)
-    where = jnp.stack([own // strip, lax.axis_index("seq") * strip + own % strip]).astype(jnp.int32)
+        return near(lax.all_to_all(values, HEAD_AXES, split_axis=0, concat_axis=0, tiled=True))
+
     (mixed,) = call(
         mix_kernel,
-        [table, whole, whole, whole],
-        [(packed_rows, span)],
+        [whole, whole, whole],
+        [(owners, KINDS, span)],
         [
+            pltpu.VMEM((2 * heads, packed_rows), bf16),
+            pltpu.VMEM((packed_rows, 2 * heads), bf16),
             pltpu.VMEM((heads, span), f32),
             pltpu.VMEM((heads, span), f32),
             pltpu.VMEM((heads, span), f32),
             pltpu.VMEM((2 * heads, span), bf16),
         ],
-        blocks=blocks, rows=rows, heads=heads, scaling=scaling,
-    )(where, exchange(packed), before, after)
+        blocks=blocks, rows=rows, strip=strip, heads=heads, scaling=scaling,
+    )(exchange(packed), mix_pre, mix_post)
 
     (sent,) = call(
         grad_kernel,
-        [table, whole, whole, whole],
+        [table, whole, whole],
         [exchange_shape],
-        [pltpu.VMEM((spread_rows, seq_len), bf16), pltpu.VMEM((KINDS, spread_rows, DH), f32)],
+        [pltpu.VMEM((spread_rows, seq_len), bf16), pltpu.VMEM((KINDS, spread_rows, DH), f32)]
+        + sorted_blocks,
         blocks=blocks, rows=rows, strip=strip,
-    )(stored_at, exchange(mixed), key_value, spread)
+    )(block_order, exchange(mixed), received)
     received = lax.all_to_all(sent, "seq", split_axis=0, concat_axis=0, tiled=True)
     summed = jnp.sum(received[:, :rows].astype(f32), axis=0).astype(bf16)
     lines = received[:, rows:].reshape(rows, 2 * width)

time: 363 us -> 347 us (0.956)
  blocking collectives: 154 us -> 334 us
  waiting for transfers between devices: 144 us -> 0 us
  starting transfers between devices: 36.2 us -> 0 us
  Pallas kernels: 16.2 us -> 6.92 us
  local copies, waits for them, and re-layouts: 9.49 us -> 4.07 us
    all_to_all x2 -> x0, waiting for transfers between devices: 144 us -> none  [the longest x1 113 us: exchange(): lax.all_to_all(values.reshape(owners, KINDS, span), HEAD_AXES, split_axis...]
    all_to_all x1 -> x2, blocking collectives: 120 us -> 264 us  [exchange(): lax.all_to_all(values, HEAD_AXES, split_axis=0, concat_axis=0, tiled=True)]
    all_to_all x1 -> x2, blocking collectives: 33.7 us -> 69.9 us  [body(): lax.all_to_all(sent, 'seq', split_axis=0, concat_axis=0, tiled=True)]
    all_to_all x2 -> x0, starting transfers between devices: 36.2 us -> none  [the longest x1 29 us: exchange(): lax.all_to_all(values.reshape(owners, KINDS, span), HEAD_AXES, split_axis...]
    reshape x7 -> x0, local copies, waits for them, and re-layouts: 7.29 us -> none  [the longest x2 3.55 us: exchange(): values.reshape(owners, KINDS, span)]
    pallas_call x3, Pallas kernels: 13.8 us -> 6.78 us  [the longest x1 2.67 us: body(): call(grad_kernel, [table, whole, whole], [exchange_shape], [pltpu.VMEM((s...]
  transfers between devices with their start and end apart: 2 -> 0, of which waited for: 2 -> 0; matrix products, arithmetic and copies ran while one was open for 1% -> 0% of each run, Pallas kernels for 0% -> 0%
where the time goes in v3:
time: 347 us; the launch traced here: 346 us
  blocking collectives  334 us (96%)
  Pallas kernels  6.92 us (2%)
  local copies, waits for them, and re-layouts  4.07 us (1%)
    all_to_all x2, blocking collectives, exchange(): lax.all_to_all(values, HEAD_AXES, split_axis=0, concat_axis=0, tiled=True)  264 us
    all_to_all x2, blocking collectives, body(): lax.all_to_all(sent, 'seq', split_axis=0, concat_axis=0, tiled=True)  69.9 us

profile of v3, /device:TPU:32, one launch (start us, length us, event | category | flops | bytes accessed | tf_op | source)
XLA Modules:
  0.0 346.1 jit_solution(9538839342136629336)
XLA Ops:
  0.6 0.0 copy-start
  0.6 0.8 copy-done
  1.5 0.0 copy-start.1
  1.5 0.8 copy-done.1
  2.3 0.0 copy-start.2
  2.3 0.8 copy-done.2
  3.2 0.0 copy-start.3
  3.2 0.8 copy-done.3
  4.0 0.1 shard_map.102
  4.1 0.0 copy-start.6
  4.2 36.7 %all_to_all.20.received_ref = bf16[16,136,512]{2,1,0:T(8,128)(2,1)S(1)} all-to-all(bf16[16,136,512]{2,1,0:T(8,128)(2,1)S(1)} %shard_map.102), channel_id=1, replica_groups=mesh['seq'=16,'row'=8,'col'=8] {'seq'}, dimensions={0} | all-to-all | bytes 4456448 | tf_op jit(solution)/shard_map/all_to_all | solution.py:245
  40.9 0.0 copy-done.6
  40.9 0.0 copy-start.4
  40.9 0.0 copy-start.5
  40.9 1.6 shard_map.103
  42.5 144.2 %all_to_all.21.incoming_ref = bf16[64,4,2176]{2,1,0:T(4,128)(2,1)S(1)} all-to-all(bf16[64,4,2176]{2,1,0:T(4,128)(2,1)S(1)} %shard_map.103), channel_id=1, replica_groups=mesh['seq'=16,'row'=8,'col'=8] {'row','col'}, dimensions={0} | all-to-all | bytes 2228224 | tf_op jit(solution)/shard_map/all_to_all | solution.py:262
  186.6 0.0 copy-done.4
  186.7 0.0 copy-done.5
  186.7 2.5 shard_map.104
  189.2 120.1 %all_to_all.22.incoming_ref = bf16[64,4,2176]{2,1,0:T(4,128)(2,1)S(1)} all-to-all(bf16[64,4,2176]{2,1,0:T(4,128)(2,1)S(1)} %shard_map.104), channel_id=1, replica_groups=mesh['seq'=16,'row'=8,'col'=8] {'row','col'}, dimensions={0} | all-to-all | bytes 2228224 | tf_op jit(solution)/shard_map/all_to_all | solution.py:262
  309.3 2.7 shard_map.105
  311.9 33.2 %all_to_all.23 = bf16[16,136,512]{2,1,0:T(8,128)(2,1)S(1)} all-to-all(bf16[16,136,512]{2,1,0:T(8,128)(2,1)S(1)} %shard_map.105), channel_id=1, replica_groups=mesh['seq'=16,'row'=8,'col'=8] {'seq'}, dimensions={0} | all-to-all | bytes 4456448 | tf_op jit(solution)/shard_map/all_to_all | solution.py:287
  345.1 0.3 slice_reduce_fusion
  345.4 0.7 fusion
  (1 shorter events, 0.0 us)
Async XLA Ops:
  0.6 0.8 copy-start
  1.5 0.8 copy-start.1
  2.3 0.8 copy-start.2
  3.2 0.8 copy-start.3
  4.1 36.7 %copy-start.6 = (s32[16]{0:T(128)S(1)}, s32[16]{0:T(128)}, u32[]{:S(2)}) copy-start(s32[16]{0:T(128)} %block_ref.3) | copy-start | bytes 196
  40.9 145.8 %copy-start.4 = (bf16[128,128]{1,0:T(8,128)(2,1)S(1)}, bf16[128,128]{1,0:T(8,128)(2,1)}, u32[]{:S(2)}) copy-start(bf16[128,128]{1,0:T(8,128)(2,1)} %pre_ref.1) | copy-start | bytes 98308
  40.9 145.8 %copy-start.5 = (bf16[128,128]{1,0:T(8,128)(2,1)S(1)}, bf16[128,128]{1,0:T(8,128)(2,1)}, u32[]{:S(2)}) copy-start(bf16[128,128]{1,0:T(8,128)(2,1)} %post_ref.1) | copy-start | bytes 98308

commit v4 on v3

v4 whole, which is shorter than its diff:
```python
import functools

import jax
import jax.numpy as jnp
from jax import lax
from jax.experimental import pallas as pl
from jax.experimental.pallas import tpu as pltpu
from jax.sharding import PartitionSpec as P

DH = 128


logit_cap = 10.0

HEAD_AXES = ("row", "col")
HEADS = 2
CHUNK = 4
VMEM_LIMIT = 24 << 20
INTERP = False
BF16, F32 = jnp.bfloat16, jnp.float32


def dot(left, right, left_dim=1, right_dim=0):
    return lax.dot_general(
        left, right, (((left_dim,), (right_dim,)), ((), ())), preferred_element_type=F32
    )


def iota(shape, dim):
    return lax.broadcasted_iota(jnp.int32, shape, dim)


def to_strips(blocks, strip):
    shape = (blocks * strip, blocks * strip)
    row, column = iota(shape, 0), iota(shape, 1)
    return jnp.where(row % strip * blocks + row // strip == column, 1.0, 0.0).astype(BF16)


def to_slots(blocks, strip):
    shape = (blocks * strip * HEADS, blocks * strip)
    row, column = iota(shape, 0), iota(shape, 1)
    block, slot = row // (strip * HEADS), row // HEADS % strip
    line = jnp.where(block < blocks // 2, slot, strip - 1 - slot)
    return jnp.where(block * strip + line == column, 1.0, 0.0).astype(BF16)


def own_head(shape):
    return iota(shape, 0) % HEADS == iota(shape, 1) // DH % HEADS


def send_kernel(
    query_hbm, key_hbm, value_hbm, grad_hbm, out_ref, query_ref, key_ref, value_ref, grad_ref, sems,
    *, blocks, rows, strip, width
):
    copies = [
        pltpu.make_async_copy(source, target, sems.at[n])
        for n, (source, target) in enumerate(
            [
                (query_hbm, query_ref),
                (grad_hbm, grad_ref),
                (key_hbm, key_ref),
                (value_hbm, value_ref),
            ]
        )
    ]
    for copy in copies:
        copy.start()
    pick = to_strips(blocks, strip)
    for copy in copies:
        copy.wait()
    queries = dot(pick, query_ref[...])
    grads = dot(pick, grad_ref[...])
    for s in range(blocks):
        out_ref[s, :rows, :width] = key_ref[...]
        out_ref[s, :rows, width:] = value_ref[...]
        out_ref[s, rows:, :width] = queries[s * strip : (s + 1) * strip, :].astype(BF16)
        out_ref[s, rows:, width:] = grads[s * strip : (s + 1) * strip, :].astype(BF16)


def sort_blocks(
    block_ref, received_ref, order_ref, key_value_ref, spread_ref, lines_ref, blocks, rows, strip
):
    for s in range(blocks):
        order_ref[block_ref[s]] = s
    for p in range(blocks):
        source = order_ref[p]
        key_value_ref[p * rows : (p + 1) * rows, :] = received_ref[source, :rows, :]
        lines_ref[p * strip : (p + 1) * strip, :] = received_ref[source, rows:, :].astype(F32)
    spread = dot(to_slots(blocks, strip), lines_ref[...].astype(BF16))
    spread_ref[...] = jnp.where(own_head(spread.shape), spread, 0.0).astype(BF16)


def score_kernel(
    block_ref, received_ref, out_ref, order_ref, key_value_ref, spread_ref, lines_ref, diagonal_ref,
    *, blocks, rows, strip, width, scaling
):
    half = blocks // 2
    group = HEADS * strip
    sort_blocks(
        block_ref, received_ref, order_ref, key_value_ref, spread_ref, lines_ref, blocks, rows, strip
    )
    for kind in range(2):
        columns = slice(kind * width, (kind + 1) * width)
        base = kind * blocks * rows
        for j in range(blocks // CHUNK):
            first = j * CHUNK
            scores = dot(
                spread_ref[first * group :, columns],
                key_value_ref[first * rows : (first + CHUNK) * rows, columns],
                1,
                1,
            )
            if kind == 0:
                scores = scores * scaling
            for p in range(first, blocks):
                piece = scores[(p - first) * group : (p - first + 1) * group, :]
                count = min(p - first, CHUNK)
                if p - first < CHUNK:
                    diagonal_ref[kind, p] = piece[:, count * rows : (count + 1) * rows]
                if count:
                    c = min(p, blocks - 1 - p)
                    lane = base + (first if p < half else blocks - 1 - p + first) * rows
                    out_ref[c * strip : (c + 1) * strip, :, lane : lane + count * rows] = (
                        piece[:, : count * rows].astype(BF16).reshape(strip, HEADS, count * rows)
                    )
    low = iota((group, rows), 1) < rows // 2
    for c in range(half):
        cut = slice(c * strip, (c + 1) * strip)
        halves = []
        for kind in range(2):
            near, far = diagonal_ref[kind, c], diagonal_ref[kind, blocks - 1 - c]
            full = jnp.concatenate([far[:strip], near[strip:]], axis=0)
            halves.append(jnp.concatenate([near[:strip], far[strip:]], axis=0))
            lane = ((kind + 1) * blocks - 1) * rows
            out_ref[cut, :, lane : lane + rows] = full.astype(BF16).reshape(strip, HEADS, rows)
        joined = jnp.where(low, halves[0], roll(halves[1], rows // 2))
        lane = 2 * blocks * rows
        out_ref[cut, :, lane:] = joined.astype(BF16).reshape(strip, HEADS, rows)


def roll(values, shift):
    if INTERP:
        return jnp.roll(values, shift, 1)
    return pltpu.roll(values, shift, 1)


def mix_kernel(
    incoming_ref, pre_ref, post_ref, out_ref, mixed_ref, grad_ref, both_ref,
    *, blocks, rows, strip, heads, scaling
):
    own = lax.axis_index(HEAD_AXES)
    pair, line = lax.div(own, strip), lax.rem(own, strip)
    seq = lax.axis_index("seq")
    near_offset = line * blocks + seq
    far_offset = (strip - 1 - line) * blocks + seq
    owners = heads // HEADS
    seq_len = blocks * rows
    pre, post = pre_ref[...], post_ref[...]
    extra = incoming_ref[:, :, 2 * seq_len :].reshape(heads, rows)
    mixed_ref[:, :seq_len] = dot(pre, incoming_ref[:, :, :seq_len].reshape(heads, seq_len))
    mixed_ref[:, seq_len:] = dot(pre, extra)
    grad_ref[:, :seq_len] = dot(
        post, incoming_ref[:, :, seq_len : 2 * seq_len].reshape(heads, seq_len), 0, 0
    )
    grad_ref[:, seq_len:] = roll(dot(post, extra, 0, 0), rows // 2)

    lane = iota((heads, rows), 1)
    early = line < strip // 2
    is_near = [j < pair for j in range(blocks - 1)]
    is_near += [jnp.logical_not(early), early]
    limits = [None] * (blocks - 1)
    limits += [jnp.where(near, near_offset, far_offset) for near in is_near[blocks - 1 :]]
    zero = jnp.zeros((heads, rows), F32)
    near_total, far_total, near_dot, far_dot = zero, zero, zero, zero
    squashed_tiles = []
    for j in range(blocks + 1):
        cut = slice(j * rows, (j + 1) * rows)
        squashed = jnp.tanh(mixed_ref[:, cut] / logit_cap)
        weights = jnp.exp(logit_cap * squashed)
        grads = grad_ref[:, cut]
        if limits[j] is not None:
            weights = jnp.where(lane <= limits[j], weights, 0.0)
        dots = weights * grads
        mixed_ref[:, cut] = weights
        grad_ref[:, cut] = grads
        squashed_tiles.append(squashed)
        near = jnp.where(is_near[j], 1.0, 0.0)
        near_total += weights * near
        far_total += weights * (1.0 - near)
        near_dot += dots * near
        far_dot += dots * (1.0 - near)

    def down(values):
        return jnp.sum(values, axis=1, keepdims=True)

    near_scale, far_scale = 1.0 / down(near_total), 1.0 / down(far_total)
    near_row, far_row = down(near_dot) * near_scale, down(far_dot) * far_scale
    for j in range(blocks + 1):
        cut = slice(j * rows, (j + 1) * rows)
        probs = mixed_ref[:, cut] * jnp.where(is_near[j], near_scale, far_scale)
        squashed = squashed_tiles[j]
        grad_capped = probs * (grad_ref[:, cut] - jnp.where(is_near[j], near_row, far_row))
        both_ref[0, :, cut] = (grad_capped * (1.0 - squashed * squashed)).astype(BF16)
        both_ref[1, :, cut] = probs.astype(BF16)
    grad_scores = dot(pre, both_ref[0], 0, 0) * scaling
    post_mixed = dot(post, both_ref[1])
    joined = jnp.where(
        lane < rows // 2, grad_scores[:, seq_len:], roll(post_mixed[:, seq_len:], rows // 2)
    )
    shape = (owners, HEADS, seq_len)
    out_ref[:, :, :seq_len] = grad_scores[:, :seq_len].astype(BF16).reshape(shape)
    out_ref[:, :, seq_len : 2 * seq_len] = post_mixed[:, :seq_len].astype(BF16).reshape(shape)
    out_ref[:, :, 2 * seq_len :] = joined.astype(BF16).reshape(owners, HEADS, rows)


def grad_kernel(
    block_ref, incoming_ref, received_ref, out_ref, dense_ref, sum_ref, order_ref, key_value_ref,
    spread_ref, lines_ref, *, blocks, rows, strip, width
):
    half = blocks // 2
    group = HEADS * strip
    sort_blocks(
        block_ref, received_ref, order_ref, key_value_ref, spread_ref, lines_ref, blocks, rows, strip
    )
    low = iota((group, rows), 1) < rows // 2
    for c in range(half):
        own = slice(c * strip, (c + 1) * strip)
        extra = incoming_ref[own, :, 2 * blocks * rows :].reshape(group, rows).astype(F32)
        for kind in range(2):
            base = kind * blocks * rows
            last = base + (blocks - 1) * rows
            full = incoming_ref[own, :, last : last + rows].reshape(group, rows).astype(F32)
            part = extra if kind == 0 else roll(extra, rows // 2)
            part = jnp.where(low, part, 0.0)
            near = jnp.concatenate([part[:strip], full[strip:]], axis=0)
            far = jnp.concatenate([full[:strip], part[strip:]], axis=0)
            for p, diagonal, lane in ((c, near, base), (blocks - 1 - c, far, base + c * rows)):
                slots = slice(p * group, (p + 1) * group)
                if p:
                    dense_ref[kind, slots, : p * rows] = incoming_ref[
                        own, :, lane : lane + p * rows
                    ].reshape(group, p * rows)
                dense_ref[kind, slots, p * rows : (p + 1) * rows] = diagonal.astype(BF16)
                reach = (p // CHUNK + 1) * CHUNK * rows
                if reach > (p + 1) * rows:
                    dense_ref[kind, slots, (p + 1) * rows : reach] = jnp.zeros(
                        (group, reach - (p + 1) * rows), BF16
                    )
    gather = to_slots(blocks, strip)
    for kind in range(2):
        columns = slice(kind * width, (kind + 1) * width)
        for j in range(blocks // CHUNK):
            first = j * CHUNK
            cut = slice(first * rows, (first + CHUNK) * rows)
            dense = dense_ref[kind, first * group :, cut]
            terms = dot(dense, spread_ref[first * group :, columns], 0, 0).astype(BF16)
            for b in range(CHUNK):
                out_ref[order_ref[first + b], :rows, columns] = terms[b * rows : (b + 1) * rows, :]
            added = dot(dense, key_value_ref[cut, columns])
            if j == 0:
                sum_ref[...] = added
            else:
                sum_ref[first * group :, :] = sum_ref[first * group :, :] + added
        found = jnp.where(own_head(sum_ref.shape), sum_ref[...], 0.0).astype(BF16)
        lines = dot(gather, found, 0, 0).astype(BF16)
        for p in range(blocks):
            out_ref[order_ref[p], rows:, columns] = lines[p * strip : (p + 1) * strip, :]


def final_kernel(
    received_ref, attended_ref, query_ref, key_ref, value_ref, lines_ref, *, blocks, rows, strip, width
):
    total = received_ref[0, :rows, :].astype(F32)
    for s in range(1, blocks):
        total += received_ref[s, :rows, :].astype(F32)
    for s in range(blocks):
        lines_ref[s * strip : (s + 1) * strip, :] = received_ref[s, rows:, :].astype(F32)
    lines = dot(to_strips(blocks, strip), lines_ref[...].astype(BF16), 0, 0).astype(BF16)
    query_ref[...] = lines[:, :width]
    attended_ref[...] = lines[:, width:]
    key_ref[...] = total[:, :width].astype(BF16)
    value_ref[...] = total[:, width:].astype(BF16)


def body(query_rows, key_rows, value_rows, out_grad, mix_pre, mix_post, block_order):
    blocks = lax.axis_size("seq")
    owners = lax.axis_size("row") * lax.axis_size("col")
    rows, width = query_rows.shape
    heads = mix_pre.shape[0]
    scaling = DH ** (-0.5)
    strip = rows // blocks
    span = (blocks + 1) * rows
    seq_len = blocks * rows
    slots = rows * HEADS
    whole = pl.BlockSpec(memory_space=pltpu.VMEM)
    table = pl.BlockSpec(memory_space=pltpu.SMEM)
    seq_shape = (blocks, rows + strip, 2 * width)
    head_shape = (owners, HEADS, (2 * blocks + 1) * rows)
    static = dict(blocks=blocks, rows=rows, strip=strip)

    def call(kernel, ins, outs, scratch=(), **more):
        return pl.pallas_call(
            functools.partial(kernel, **static, **more),
            in_specs=ins,
            out_specs=[whole] * len(outs),
            out_shape=[jax.ShapeDtypeStruct(shape, BF16) for shape in outs],
            scratch_shapes=scratch,
            compiler_params=pltpu.CompilerParams(vmem_limit_bytes=VMEM_LIMIT),
            interpret=INTERP,
        )

    def exchange(values, axes):
        values = lax.all_to_all(values, axes, split_axis=0, concat_axis=0, tiled=True)
        if INTERP:
            return values
        return pltpu.with_memory_space_constraint(values, pltpu.VMEM)

    def far(values):
        return values if INTERP else pltpu.with_memory_space_constraint(values, pltpu.HBM)

    (sent,) = call(
        send_kernel,
        [pl.BlockSpec(memory_space=pltpu.HBM)] * 4,
        [seq_shape],
        [pltpu.VMEM((rows, width), BF16)] * 4 + [pltpu.SemaphoreType.DMA((4,))],
        width=width,
    )(*[far(values) for values in (query_rows, key_rows, value_rows, out_grad)])
    received = exchange(sent, "seq")
    sorted_blocks = [
        pltpu.SMEM((blocks,), jnp.int32),
        pltpu.VMEM((seq_len, 2 * width), BF16),
        pltpu.VMEM((slots, 2 * width), BF16),
        pltpu.VMEM((rows, 2 * width), F32),
    ]
    (packed,) = call(
        score_kernel,
        [table, whole],
        [head_shape],
        sorted_blocks + [pltpu.VMEM((2, blocks, HEADS * strip, rows), F32)],
        width=width, scaling=scaling,
    )(block_order, received)
    (mixed,) = call(
        mix_kernel,
        [whole] * 3,
        [head_shape],
        [
            pltpu.VMEM((heads, span), F32),
            pltpu.VMEM((heads, span), F32),
            pltpu.VMEM((2, heads, span), BF16),
        ],
        heads=heads, scaling=scaling,
    )(exchange(packed, HEAD_AXES), mix_pre, mix_post)
    (sent,) = call(
        grad_kernel,
        [table, whole, whole],
        [seq_shape],
        [pltpu.VMEM((2, slots, seq_len), BF16), pltpu.VMEM((slots, width), F32)] + sorted_blocks,
        width=width,
    )(block_order, exchange(mixed, HEAD_AXES), received)
    return call(
        final_kernel,
        [whole],
        [(rows, width)] * 4,
        [pltpu.VMEM((rows, 2 * width), F32)],
        width=width,
    )(exchange(sent, "seq"))


def solution(mesh):
    spread = P("seq", HEAD_AXES)
    return jax.shard_map(
        body,
        mesh=mesh,
        in_specs=(spread, spread, spread, spread, P(), P(), P()),
        out_specs=(spread, spread, spread, spread),
        check_vma=False,
    )
```

time: 347 us -> 337 us (0.971)
  blocking collectives: 334 us -> 328 us
  local copies, waits for them, and re-layouts: 4.07 us -> 0.01 us
    all_to_all x4, blocking collectives: 334 us -> 328 us  [exchange(): lax.all_to_all(values, axes, split_axis=0, concat_axis=0, tiled=True)]
    pallas_call x4 -> x5, Pallas kernels: 6.92 us -> 7.79 us  [the longest x1 2.16 us: body(): call(grad_kernel, [table, whole, whole], [seq_shape], [pltpu.VMEM((2, slo...]
where the time goes in v4:
time: 337 us
  blocking collectives  328 us (97%)
  Pallas kernels  7.79 us (2%)
    all_to_all x4, blocking collectives, exchange(): lax.all_to_all(values, axes, split_axis=0, concat_axis=0, tiled=True)  328 us

profile of v4, /device:TPU:32, one launch (start us, length us, event | category | flops | bytes accessed | tf_op | source)
XLA Modules:
  0.0 336.6 jit_solution(10938531877617866949)
XLA Ops:
  0.6 1.3 shard_map.102
  1.9 0.0 copy-start.2
  1.9 36.7 %all_to_all.20.received_ref = bf16[16,136,512]{2,1,0:T(8,128)(2,1)S(1)} all-to-all(bf16[16,136,512]{2,1,0:T(8,128)(2,1)S(1)} %shard_map.102), channel_id=1, replica_groups=mesh['seq'=16,'row'=8,'col'=8] {'seq'}, dimensions={0} | all-to-all | bytes 4456448 | tf_op jit(solution)/shard_map/all_to_all | solution.py:313
  38.6 0.0 copy-done.2
  38.6 0.0 copy-start
  38.6 0.0 copy-start.1
  38.6 1.5 shard_map.103
  40.2 141.4 %all_to_all.21.incoming_ref = bf16[64,2,4224]{2,1,0:T(2,128)(2,1)S(1)} all-to-all(bf16[64,2,4224]{2,1,0:T(2,128)(2,1)S(1)} %shard_map.103), channel_id=1, replica_groups=mesh['seq'=16,'row'=8,'col'=8] {'row','col'}, dimensions={0} | all-to-all | bytes 2162688 | tf_op jit(solution)/shard_map/all_to_all | solution.py:313
  181.5 0.0 copy-done
  181.5 0.0 copy-done.1
  181.5 1.8 shard_map.104
  183.3 117.3 %all_to_all.22.incoming_ref = bf16[64,2,4224]{2,1,0:T(2,128)(2,1)S(1)} all-to-all(bf16[64,2,4224]{2,1,0:T(2,128)(2,1)S(1)} %shard_map.104), channel_id=1, replica_groups=mesh['seq'=16,'row'=8,'col'=8] {'row','col'}, dimensions={0} | all-to-all | bytes 2162688 | tf_op jit(solution)/shard_map/all_to_all | solution.py:313
  300.6 2.2 shard_map.105
  302.8 32.8 %all_to_all.23.received_ref = bf16[16,136,512]{2,1,0:T(8,128)(2,1)S(1)} all-to-all(bf16[16,136,512]{2,1,0:T(8,128)(2,1)S(1)} %shard_map.105), channel_id=1, replica_groups=mesh['seq'=16,'row'=8,'col'=8] {'seq'}, dimensions={0} | all-to-all | bytes 4456448 | tf_op jit(solution)/shard_map/all_to_all | solution.py:313
  335.5 1.1 shard_map.106
Async XLA Ops:
  1.9 36.7 %copy-start.2 = (s32[16]{0:T(128)S(1)}, s32[16]{0:T(128)}, u32[]{:S(2)}) copy-start(s32[16]{0:T(128)} %block_ref.3) | copy-start | bytes 196
  38.6 142.9 %copy-start = (bf16[128,128]{1,0:T(8,128)(2,1)S(1)}, bf16[128,128]{1,0:T(8,128)(2,1)}, u32[]{:S(2)}) copy-start(bf16[128,128]{1,0:T(8,128)(2,1)} %pre_ref.1) | copy-start | bytes 98308
  38.6 142.9 %copy-start.1 = (bf16[128,128]{1,0:T(8,128)(2,1)S(1)}, bf16[128,128]{1,0:T(8,128)(2,1)}, u32[]{:S(2)}) copy-start(bf16[128,128]{1,0:T(8,128)(2,1)} %post_ref.1) | copy-start | bytes 98308

commit v5 on v4

v5 whole, which is shorter than its diff:
```python
import functools

import jax
import jax.numpy as jnp
from jax import lax
from jax.experimental import pallas as pl
from jax.experimental.pallas import tpu as pltpu
from jax.sharding import PartitionSpec as P

DH = 128


logit_cap = 10.0

HEAD_AXES = ("row", "col")
HEADS = 2
CHUNK = 2
SPLIT = 2
VMEM_LIMIT = 24 << 20
INTERP = False
BF16, F32 = jnp.bfloat16, jnp.float32


def dot(left, right, left_dim=1, right_dim=0):
    return lax.dot_general(
        left, right, (((left_dim,), (right_dim,)), ((), ())), preferred_element_type=F32
    )


def iota(shape, dim):
    return lax.broadcasted_iota(jnp.int32, shape, dim)


def to_classes(rows, classes):
    row, column = iota((rows, rows), 0), iota((rows, rows), 1)
    per = rows // classes
    return jnp.where(row % per * classes + row // per == column, 1.0, 0.0).astype(BF16)


def to_slots(supers, reach):
    shape = (supers * reach * HEADS, supers * reach)
    row, column = iota(shape, 0), iota(shape, 1)
    block, slot = row // (reach * HEADS), row // HEADS % reach
    line = jnp.where(block < supers // 2, slot, reach - 1 - slot)
    return jnp.where(block * reach + line == column, 1.0, 0.0).astype(BF16)


def own_head(shape):
    return iota(shape, 0) % HEADS == iota(shape, 1) // DH % HEADS


def send_kernel(
    query_hbm, key_hbm, value_hbm, grad_hbm, out_ref, query_ref, key_ref, value_ref, grad_ref, sems,
    *, blocks, rows, strip, width
):
    copies = [
        pltpu.make_async_copy(source, target, sems.at[n])
        for n, (source, target) in enumerate(
            [
                (query_hbm, query_ref),
                (grad_hbm, grad_ref),
                (key_hbm, key_ref),
                (value_hbm, value_ref),
            ]
        )
    ]
    for copy in copies:
        copy.start()
    pick_keys, pick_lines = to_classes(rows, SPLIT), to_classes(rows, blocks // SPLIT)
    for copy in copies:
        copy.wait()
    queries = dot(pick_lines, query_ref[...]).astype(BF16)
    grads = dot(pick_lines, grad_ref[...]).astype(BF16)
    keys = dot(pick_keys, key_ref[...]).astype(BF16)
    values = dot(pick_keys, value_ref[...]).astype(BF16)
    part = rows // SPLIT
    for s in range(blocks):
        key_cut = slice(s % SPLIT * part, (s % SPLIT + 1) * part)
        line_cut = slice(s // SPLIT * strip, (s // SPLIT + 1) * strip)
        out_ref[s, :part, :width] = keys[key_cut, :]
        out_ref[s, :part, width:] = values[key_cut, :]
        out_ref[s, part:, :width] = queries[line_cut, :]
        out_ref[s, part:, width:] = grads[line_cut, :]


def sort_blocks(
    block_ref, received_ref, order_ref, key_value_ref, spread_ref, lines_ref, blocks, rows, strip
):
    part = rows // SPLIT
    for s in range(blocks):
        order_ref[block_ref[s]] = s
    for p in range(blocks):
        source = order_ref[p]
        key_value_ref[p * part : (p + 1) * part, :] = received_ref[source, :part, :]
        lines_ref[p * strip : (p + 1) * strip, :] = received_ref[source, part:, :].astype(F32)
    spread = dot(to_slots(blocks // SPLIT, strip * SPLIT), lines_ref[...].astype(BF16))
    spread_ref[...] = jnp.where(own_head(spread.shape), spread, 0.0).astype(BF16)


def score_kernel(
    block_ref, received_ref, out_ref, order_ref, key_value_ref, spread_ref, lines_ref, diagonal_ref,
    *, blocks, rows, strip, width, scaling
):
    supers = blocks // SPLIT
    half = supers // 2
    per = strip * SPLIT // 2
    side = per * HEADS
    group = 2 * side
    tiles = 2 * supers + 1
    sort_blocks(
        block_ref, received_ref, order_ref, key_value_ref, spread_ref, lines_ref, blocks, rows, strip
    )
    for kind in range(2):
        columns = slice(kind * width, (kind + 1) * width)
        for j in range(supers // CHUNK):
            first = j * CHUNK
            scores = dot(
                spread_ref[first * group :, columns],
                key_value_ref[first * rows : (first + CHUNK) * rows, columns],
                1,
                1,
            )
            if kind == 0:
                scores = scores * scaling
            for p in range(first, supers):
                piece = scores[(p - first) * group : (p - first + 1) * group, :]
                count = min(p - first, CHUNK)
                if p - first < CHUNK:
                    diagonal_ref[kind, p] = piece[:, count * rows : (count + 1) * rows]
                if count:
                    c = min(p, supers - 1 - p)
                    skip = kind * supers + (first if p < half else supers - 1 - p + first)
                    for u in range(2):
                        lane = (u * tiles + skip) * rows
                        out_ref[c * per : (c + 1) * per, :, lane : lane + count * rows] = (
                            piece[u * side : (u + 1) * side, : count * rows]
                            .astype(BF16)
                            .reshape(per, HEADS, count * rows)
                        )
    low = iota((side, rows), 1) < rows // 2
    for c in range(half):
        cut = slice(c * per, (c + 1) * per)
        for u in range(2):
            own = slice(u * side, (u + 1) * side)
            halves = []
            for kind in range(2):
                near = diagonal_ref[kind, c, own]
                far = diagonal_ref[kind, supers - 1 - c, own]
                full, part = (near, far) if u else (far, near)
                halves.append(part)
                lane = (u * tiles + (kind + 1) * supers - 1) * rows
                out_ref[cut, :, lane : lane + rows] = full.astype(BF16).reshape(per, HEADS, rows)
            joined = jnp.where(low, halves[0], roll(halves[1], rows // 2))
            lane = (u * tiles + 2 * supers) * rows
            out_ref[cut, :, lane : lane + rows] = joined.astype(BF16).reshape(per, HEADS, rows)


def roll(values, shift):
    if INTERP:
        return jnp.roll(values, shift, 1)
    return pltpu.roll(values, shift, 1)


def near_tiles(pair, supers, u):
    return [j < pair for j in range(supers - 1)] + [u == 1, u == 0]


def weigh_kernel(
    incoming_ref, pre_ref, post_ref, weight_ref, squashed_ref, grad_ref, sum_ref,
    *, blocks, rows, strip, heads
):
    supers = blocks // SPLIT
    per = strip * SPLIT // 2
    own = lax.axis_index(HEAD_AXES)
    pair, slot = lax.div(own, per), lax.rem(own, per)
    seq = lax.axis_index("seq")
    line_class, key_class = lax.div(seq, SPLIT), lax.rem(seq, SPLIT)
    pre, post = pre_ref[...], post_ref[...]
    lane = iota((heads, rows), 1)
    full = supers * rows
    sums = jnp.zeros((heads, rows), F32)
    for u in range(2):
        base = u * (2 * supers + 1) * rows
        mine = u * (supers + 1) * rows
        extra = incoming_ref[:, :, base + 2 * full : base + 2 * full + rows].reshape(heads, rows)
        squashed_ref[:, mine : mine + full] = dot(
            pre, incoming_ref[:, :, base : base + full].reshape(heads, full)
        )
        squashed_ref[:, mine + full : mine + full + rows] = dot(pre, extra)
        grad_ref[:, mine : mine + full] = dot(
            post, incoming_ref[:, :, base + full : base + 2 * full].reshape(heads, full), 0, 0
        )
        grad_ref[:, mine + full : mine + full + rows] = roll(dot(post, extra, 0, 0), rows // 2)
        line = slot + u * per
        limits = []
        for at in (line, 2 * per - 1 - line):
            offset = at * (blocks // SPLIT) + line_class
            limits.append(lax.div(offset - key_class + SPLIT, SPLIT) - 1)
        is_near = near_tiles(pair, supers, u)
        zero = jnp.zeros((heads, rows), F32)
        parts = [zero, zero, zero, zero]
        for j in range(supers + 1):
            cut = slice(mine + j * rows, mine + (j + 1) * rows)
            squashed = jnp.tanh(squashed_ref[:, cut] / logit_cap)
            weights = jnp.exp(logit_cap * squashed)
            if j >= supers - 1:
                weights = jnp.where(lane <= limits[0 if is_near[j] else 1], weights, 0.0)
            squashed_ref[:, cut] = squashed
            weight_ref[:, cut] = weights
            dots = weights * grad_ref[:, cut]
            near = jnp.where(is_near[j], 1.0, 0.0)
            for n, values in enumerate((weights, dots)):
                parts[2 * n] += values * near
                parts[2 * n + 1] += values * (1.0 - near)
        for n, values in enumerate(parts):
            down = jnp.sum(values, axis=1, keepdims=True)
            sums += jnp.where(lane == 4 * u + n, down, 0.0)
    sum_ref[...] = sums


def mix_kernel(
    weight_ref, squashed_ref, grad_ref, own_ref, other_ref, pre_ref, post_ref, out_ref, both_ref,
    *, blocks, rows, strip, heads, scaling
):
    supers = blocks // SPLIT
    per = strip * SPLIT // 2
    pair = lax.div(lax.axis_index(HEAD_AXES), per)
    owners = heads // HEADS
    full = supers * rows
    pre, post = pre_ref[...], post_ref[...]
    lane = iota((heads, rows), 1)
    sums = own_ref[...] + other_ref[...]
    for u in range(2):
        base = u * (2 * supers + 1) * rows
        mine = u * (supers + 1) * rows
        near_total, far_total, near_dot, far_dot = [
            jnp.sum(jnp.where(lane == 4 * u + n, sums, 0.0), axis=1, keepdims=True)
            for n in range(4)
        ]
        near_scale, far_scale = 1.0 / near_total, 1.0 / far_total
        near_row, far_row = near_dot * near_scale, far_dot * far_scale
        is_near = near_tiles(pair, supers, u)
        for j in range(supers + 1):
            cut = slice(mine + j * rows, mine + (j + 1) * rows)
            probs = weight_ref[:, cut] * jnp.where(is_near[j], near_scale, far_scale)
            squashed = squashed_ref[:, cut]
            grad_capped = probs * (grad_ref[:, cut] - jnp.where(is_near[j], near_row, far_row))
            both_ref[0, :, cut] = (grad_capped * (1.0 - squashed * squashed)).astype(BF16)
            both_ref[1, :, cut] = probs.astype(BF16)
        cut = slice(mine, mine + full + rows)
        grad_scores = dot(pre, both_ref[0, :, cut], 0, 0) * scaling
        post_mixed = dot(post, both_ref[1, :, cut])
        joined = jnp.where(
            lane < rows // 2, grad_scores[:, full:], roll(post_mixed[:, full:], rows // 2)
        )
        shape = (owners, HEADS, full)
        out_ref[:, :, base : base + full] = grad_scores[:, :full].astype(BF16).reshape(shape)
        out_ref[:, :, base + full : base + 2 * full] = (
            post_mixed[:, :full].astype(BF16).reshape(shape)
        )
        out_ref[:, :, base + 2 * full : base + 2 * full + rows] = joined.astype(BF16).reshape(
            owners, HEADS, rows
        )


def grad_kernel(
    block_ref, incoming_ref, received_ref, out_ref, dense_ref, sum_ref, order_ref, key_value_ref,
    spread_ref, lines_ref, *, blocks, rows, strip, width
):
    supers = blocks // SPLIT
    half = supers // 2
    per = strip * SPLIT // 2
    side = per * HEADS
    group = 2 * side
    tiles = 2 * supers + 1
    part = rows // SPLIT
    sort_blocks(
        block_ref, received_ref, order_ref, key_value_ref, spread_ref, lines_ref, blocks, rows, strip
    )
    low = iota((side, rows), 1) < rows // 2
    for c in range(half):
        own = slice(c * per, (c + 1) * per)
        for u in range(2):
            lane = (u * tiles + 2 * supers) * rows
            extra = incoming_ref[own, :, lane : lane + rows].reshape(side, rows).astype(F32)
            for kind in range(2):
                base = (u * tiles + kind * supers) * rows
                last = base + (supers - 1) * rows
                full = incoming_ref[own, :, last : last + rows].reshape(side, rows)
                rest = extra if kind == 0 else roll(extra, rows // 2)
                rest = jnp.where(low, rest, 0.0).astype(BF16)
                near, far = (full, rest) if u else (rest, full)
                for p, diagonal, lane in ((c, near, base), (supers - 1 - c, far, base + c * rows)):
                    slots = slice(p * group + u * side, p * group + (u + 1) * side)
                    if p:
                        dense_ref[kind, slots, : p * rows] = incoming_ref[
                            own, :, lane : lane + p * rows
                        ].reshape(side, p * rows)
                    dense_ref[kind, slots, p * rows : (p + 1) * rows] = diagonal
                    to = (p // CHUNK + 1) * CHUNK * rows
                    if to > (p + 1) * rows:
                        dense_ref[kind, slots, (p + 1) * rows : to] = jnp.zeros(
                            (side, to - (p + 1) * rows), BF16
                        )
    gather = to_slots(supers, 2 * per)
    for kind in range(2):
        columns = slice(kind * width, (kind + 1) * width)
        for j in range(supers // CHUNK):
            first = j * CHUNK
            cut = slice(first * rows, (first + CHUNK) * rows)
            dense = dense_ref[kind, first * group :, cut]
            terms = dot(dense, spread_ref[first * group :, columns], 0, 0).astype(BF16)
            for b in range(CHUNK * SPLIT):
                out_ref[order_ref[first * SPLIT + b], :part, columns] = terms[
                    b * part : (b + 1) * part, :
                ]
            added = dot(dense, key_value_ref[cut, columns])
            if j == 0:
                sum_ref[...] = added
            else:
                sum_ref[first * group :, :] = sum_ref[first * group :, :] + added
        found = jnp.where(own_head(sum_ref.shape), sum_ref[...], 0.0).astype(BF16)
        lines = dot(gather, found, 0, 0).astype(BF16)
        for p in range(blocks):
            out_ref[order_ref[p], part:, columns] = lines[p * strip : (p + 1) * strip, :]


def final_kernel(
    received_ref, attended_ref, query_ref, key_ref, value_ref, keys_ref, lines_ref,
    *, blocks, rows, strip, width
):
    part = rows // SPLIT
    for k in range(SPLIT):
        total = received_ref[k, :part, :].astype(F32)
        for s in range(k + SPLIT, blocks, SPLIT):
            total += received_ref[s, :part, :].astype(F32)
        keys_ref[k * part : (k + 1) * part, :] = total.astype(BF16)
    for n in range(blocks // SPLIT):
        total = received_ref[n * SPLIT, part:, :].astype(F32)
        for k in range(1, SPLIT):
            total += received_ref[n * SPLIT + k, part:, :].astype(F32)
        lines_ref[n * strip : (n + 1) * strip, :] = total
    lines = dot(to_classes(rows, blocks // SPLIT), lines_ref[...].astype(BF16), 0, 0).astype(BF16)
    keys = dot(to_classes(rows, SPLIT), keys_ref[...], 0, 0).astype(BF16)
    query_ref[...] = lines[:, :width]
    attended_ref[...] = lines[:, width:]
    key_ref[...] = keys[:, :width]
    value_ref[...] = keys[:, width:]


def body(query_rows, key_rows, value_rows, out_grad, mix_pre, mix_post, block_order):
    blocks = lax.axis_size("seq")
    owners = lax.axis_size("row") * lax.axis_size("col")
    rows, width = query_rows.shape
    heads = mix_pre.shape[0]
    scaling = DH ** (-0.5)
    strip = rows // blocks * SPLIT
    supers = blocks // SPLIT
    span = 2 * (supers + 1) * rows
    keys = supers * rows
    lines = blocks * strip
    slots = lines * HEADS
    whole = pl.BlockSpec(memory_space=pltpu.VMEM)
    table = pl.BlockSpec(memory_space=pltpu.SMEM)
    seq_shape = (blocks, rows // SPLIT + strip, 2 * width)
    head_shape = (owners, HEADS, 2 * (2 * supers + 1) * rows)
    static = dict(blocks=blocks, rows=rows, strip=strip)

    def call(kernel, ins, outs, scratch=(), dtype=BF16, **more):
        return pl.pallas_call(
            functools.partial(kernel, **static, **more),
            in_specs=ins,
            out_specs=[whole] * len(outs),
            out_shape=[jax.ShapeDtypeStruct(shape, dtype) for shape in outs],
            scratch_shapes=scratch,
            compiler_params=pltpu.CompilerParams(vmem_limit_bytes=VMEM_LIMIT),
            interpret=INTERP,
        )

    def exchange(values, axes):
        return near(lax.all_to_all(values, axes, split_axis=0, concat_axis=0, tiled=True))

    def near(values):
        return values if INTERP else pltpu.with_memory_space_constraint(values, pltpu.VMEM)

    def far(values):
        return values if INTERP else pltpu.with_memory_space_constraint(values, pltpu.HBM)

    (sent,) = call(
        send_kernel,
        [pl.BlockSpec(memory_space=pltpu.HBM)] * 4,
        [seq_shape],
        [pltpu.VMEM((rows, width), BF16)] * 4 + [pltpu.SemaphoreType.DMA((4,))],
        width=width,
    )(*[far(values) for values in (query_rows, key_rows, value_rows, out_grad)])
    received = exchange(sent, "seq")
    sorted_blocks = [
        pltpu.SMEM((blocks,), jnp.int32),
        pltpu.VMEM((keys, 2 * width), BF16),
        pltpu.VMEM((slots, 2 * width), BF16),
        pltpu.VMEM((lines, 2 * width), F32),
    ]
    (packed,) = call(
        score_kernel,
        [table, whole],
        [head_shape],
        sorted_blocks + [pltpu.VMEM((2, supers, HEADS * strip * SPLIT, rows), F32)],
        width=width, scaling=scaling,
    )(block_order, received)
    weights, squashed, grads, sums = call(
        weigh_kernel,
        [whole] * 3,
        [(heads, span)] * 3 + [(heads, rows)],
        dtype=F32, heads=heads,
    )(exchange(packed, HEAD_AXES), mix_pre, mix_post)
    others = lax.ppermute(sums, "seq", [(s, s ^ 1) for s in range(blocks)])
    (mixed,) = call(
        mix_kernel,
        [whole] * 7,
        [head_shape],
        [pltpu.VMEM((2, heads, span), BF16)],
        heads=heads, scaling=scaling,
    )(near(weights), near(squashed), near(grads), sums, near(others), mix_pre, mix_post)
    (sent,) = call(
        grad_kernel,
        [table, whole, whole],
        [seq_shape],
        [pltpu.VMEM((2, slots, keys), BF16), pltpu.VMEM((slots, width), F32)] + sorted_blocks,
        width=width,
    )(block_order, exchange(mixed, HEAD_AXES), received)
    return call(
        final_kernel,
        [whole],
        [(rows, width)] * 4,
        [pltpu.VMEM((rows, 2 * width), BF16), pltpu.VMEM((rows, 2 * width), F32)],
        width=width,
    )(exchange(sent, "seq"))


def solution(mesh):
    spread = P("seq", HEAD_AXES)
    return jax.shard_map(
        body,
        mesh=mesh,
        in_specs=(spread, spread, spread, spread, P(), P(), P()),
        out_specs=(spread, spread, spread, spread),
        check_vma=False,
    )
```

time: 337 us -> 329 us (0.976)
  blocking collectives: 328 us -> 314 us
  waiting for transfers between devices: 0 us -> 3.84 us
    all_to_all x4, blocking collectives: 328 us -> 314 us  [exchange(): lax.all_to_all(values, axes, split_axis=0, concat_axis=0, tiled=True)]
    ppermute x0 -> x1, waiting for transfers between devices: none -> 3.84 us  [body(): others = lax.ppermute(sums, 'seq', [(s, s ^ 1) for s in range(blocks)])]
  transfers between devices with their start and end apart: 0 -> 1, of which waited for: 0 -> 1; matrix products, arithmetic and copies ran while one was open for 0% -> 0% of each run, Pallas kernels for 0% -> 0%
where the time goes in v5:
time: 329 us
  blocking collectives  314 us (95%)
  Pallas kernels  8.05 us (2%)
  waiting for transfers between devices  3.84 us (1%)
    all_to_all x4, blocking collectives, exchange(): lax.all_to_all(values, axes, split_axis=0, concat_axis=0, tiled=True)  314 us
  transfers between devices with their start and end apart: 1, of which 1 were waited for; matrix products, arithmetic and copies ran while one was open for 0% of the time, Pallas kernels for 0%

profile of v5, /device:TPU:32, one launch (start us, length us, event | category | flops | bytes accessed | tf_op | source)
XLA Modules:
  0.0 328.9 jit_solution(13261814511985489956)
XLA Ops:
  0.6 1.2 shard_map.102
  1.9 0.0 copy-start.2
  1.9 26.6 %all_to_all.20.received_ref = bf16[16,80,512]{2,1,0:T(8,128)(2,1)S(1)} all-to-all(bf16[16,80,512]{2,1,0:T(8,128)(2,1)S(1)} %shard_map.102), channel_id=1, replica_groups=mesh['seq'=16,'row'=8,'col'=8] {'seq'}, dimensions={0} | all-to-all | bytes 2621440 | tf_op jit(solution)/shard_map/all_to_all | solution.py:381
  28.4 0.0 copy-done.2
  28.4 1.5 shard_map.103
  29.9 0.0 copy-start
  29.9 0.0 copy-start.1
  29.9 144.2 %all_to_all.21.incoming_ref = bf16[64,2,4352]{2,1,0:T(2,128)(2,1)S(1)} all-to-all(bf16[64,2,4352]{2,1,0:T(2,128)(2,1)S(1)} %shard_map.103), channel_id=1, replica_groups=mesh['seq'=16,'row'=8,'col'=8] {'row','col'}, dimensions={0} | all-to-all | bytes 2228224 | tf_op jit(solution)/shard_map/all_to_all | solution.py:381
  174.1 0.0 copy-done
  174.1 0.0 copy-done.1
  174.1 1.0 shard_map.104
  175.1 2.3 collective-permute-start
  177.4 3.8 %collective-permute-done.other_ref = f32[128,128]{1,0:T(8,128)S(1)} collective-permute-done((f32[128,128]{1,0:T(8,128)S(1)}, f32[128,128]{1,0:T(8,128)S(1)}, u32[]{:S(2)}, u32[]{:S(2)}) %collective-permute-start) | collective-permute-done | bytes 65568 | tf_op jit(solution)/shard_map/ppermute | solution.py:416
  181.2 1.0 shard_map.105
  182.3 120.1 %all_to_all.22.incoming_ref = bf16[64,2,4352]{2,1,0:T(2,128)(2,1)S(1)} all-to-all(bf16[64,2,4352]{2,1,0:T(2,128)(2,1)S(1)} %shard_map.105), channel_id=1, replica_groups=mesh['seq'=16,'row'=8,'col'=8] {'row','col'}, dimensions={0} | all-to-all | bytes 2228224 | tf_op jit(solution)/shard_map/all_to_all | solution.py:381
  302.4 2.4 shard_map.106
  304.8 23.2 %all_to_all.23.received_ref = bf16[16,80,512]{2,1,0:T(8,128)(2,1)S(1)} all-to-all(bf16[16,80,512]{2,1,0:T(8,128)(2,1)S(1)} %shard_map.106), channel_id=1, replica_groups=mesh['seq'=16,'row'=8,'col'=8] {'seq'}, dimensions={0} | all-to-all | bytes 2621440 | tf_op jit(solution)/shard_map/all_to_all | solution.py:381
  327.9 1.0 shard_map.107
Async XLA Ops:
  1.9 26.6 %copy-start.2 = (s32[16]{0:T(128)S(1)}, s32[16]{0:T(128)}, u32[]{:S(2)}) copy-start(s32[16]{0:T(128)} %block_ref.3) | copy-start | bytes 196
  29.9 144.2 %copy-start = (bf16[128,128]{1,0:T(8,128)(2,1)S(1)}, bf16[128,128]{1,0:T(8,128)(2,1)}, u32[]{:S(2)}) copy-start(bf16[128,128]{1,0:T(8,128)(2,1)} %pre_ref.3) | copy-start | bytes 98308
  29.9 144.2 %copy-start.1 = (bf16[128,128]{1,0:T(8,128)(2,1)S(1)}, bf16[128,128]{1,0:T(8,128)(2,1)}, u32[]{:S(2)}) copy-start(bf16[128,128]{1,0:T(8,128)(2,1)} %post_ref.3) | copy-start | bytes 98308
  175.1 6.2 %collective-permute-start = (f32[128,128]{1,0:T(8,128)S(1)}, f32[128,128]{1,0:T(8,128)S(1)}, u32[]{:S(2)}, u32[]{:S(2)}) collective-permute-start(f32[128,128]{1,0:T(8,128)S(1)} %get-tuple-element.11.own_ref), channel_id=1, source_target_pairs={{0,64},{64,0},{128,192},{192,128},{256,320},{320,256},{384,448},{4... | collective-permute-start | bytes 196616 | tf_op jit(solution)/shard_map/ppermute | solution.py:416

commit v6 on v5

--- a/solution.py
+++ b/solution.py
@@ -106,7 +106,6 @@
     per = strip * SPLIT // 2
     side = per * HEADS
     group = 2 * side
-    tiles = 2 * supers + 1
     sort_blocks(
         block_ref, received_ref, order_ref, key_value_ref, spread_ref, lines_ref, blocks, rows, strip
     )
@@ -131,31 +130,42 @@
                     c = min(p, supers - 1 - p)
                     skip = kind * supers + (first if p < half else supers - 1 - p + first)
                     for u in range(2):
-                        lane = (u * tiles + skip) * rows
+                        lane = (2 * u * supers + skip) * rows
                         out_ref[c * per : (c + 1) * per, :, lane : lane + count * rows] = (
                             piece[u * side : (u + 1) * side, : count * rows]
                             .astype(BF16)
                             .reshape(per, HEADS, count * rows)
                         )
-    low = iota((side, rows), 1) < rows // 2
+    lane_of = iota((side, rows), 1)
     for c in range(half):
         cut = slice(c * per, (c + 1) * per)
+        shared = jnp.zeros((side, rows), F32)
         for u in range(2):
             own = slice(u * side, (u + 1) * side)
-            halves = []
+            taken = blended(side, rows, u)
             for kind in range(2):
                 near = diagonal_ref[kind, c, own]
                 far = diagonal_ref[kind, supers - 1 - c, own]
-                full, part = (near, far) if u else (far, near)
-                halves.append(part)
-                lane = (u * tiles + (kind + 1) * supers - 1) * rows
+                late, early = (near, far) if u else (far, near)
+                full = jnp.where(taken, roll(early, rows // 2), late)
+                lane = (2 * u * supers + (kind + 1) * supers - 1) * rows
                 out_ref[cut, :, lane : lane + rows] = full.astype(BF16).reshape(per, HEADS, rows)
-            joined = jnp.where(low, halves[0], roll(halves[1], rows // 2))
-            lane = (u * tiles + 2 * supers) * rows
-            out_ref[cut, :, lane : lane + rows] = joined.astype(BF16).reshape(per, HEADS, rows)
+                quarter = 2 * u + kind
+                shared = jnp.where(
+                    lane_of // (rows // 4) == quarter, roll(early, quarter * rows // 4), shared
+                )
+        out_ref[cut, :, 4 * supers * rows :] = shared.astype(BF16).reshape(per, HEADS, rows)
+
+
+def blended(side, rows, u):
+    late_slot = iota((side, rows), 0) >= side // 2
+    return (iota((side, rows), 1) >= rows * 3 // 4) & (late_slot if u == 0 else ~late_slot)
 
 
 def roll(values, shift):
+    shift %= values.shape[1]
+    if shift == 0:
+        return values
     if INTERP:
         return jnp.roll(values, shift, 1)
     return pltpu.roll(values, shift, 1)
@@ -163,6 +173,12 @@
 
 def near_tiles(pair, supers, u):
     return [j < pair for j in range(supers - 1)] + [u == 1, u == 0]
+
+
+def early_lanes(lane, slot, per, u):
+    start = lane.shape[1] * 3 // 4
+    blend = slot >= per // 2 if u == 0 else slot < per // 2
+    return lane >= jnp.where(blend, start, lane.shape[1])
 
 
 def weigh_kernel(
@@ -179,23 +195,30 @@
     lane = iota((heads, rows), 1)
     full = supers * rows
     sums = jnp.zeros((heads, rows), F32)
+    shared = incoming_ref[:, :, 4 * full :].reshape(heads, rows)
+    shared_mixed, shared_grads = dot(pre, shared), dot(post, shared, 0, 0)
     for u in range(2):
-        base = u * (2 * supers + 1) * rows
+        base = 2 * u * full
         mine = u * (supers + 1) * rows
-        extra = incoming_ref[:, :, base + 2 * full : base + 2 * full + rows].reshape(heads, rows)
         squashed_ref[:, mine : mine + full] = dot(
             pre, incoming_ref[:, :, base : base + full].reshape(heads, full)
         )
-        squashed_ref[:, mine + full : mine + full + rows] = dot(pre, extra)
+        squashed_ref[:, mine + full : mine + full + rows] = roll(
+            shared_mixed, -2 * u * (rows // 4)
+        )
         grad_ref[:, mine : mine + full] = dot(
             post, incoming_ref[:, :, base + full : base + 2 * full].reshape(heads, full), 0, 0
         )
-        grad_ref[:, mine + full : mine + full + rows] = roll(dot(post, extra, 0, 0), rows // 2)
+        grad_ref[:, mine + full : mine + full + rows] = roll(
+            shared_grads, -(2 * u + 1) * (rows // 4)
+        )
         line = slot + u * per
         limits = []
         for at in (line, 2 * per - 1 - line):
             offset = at * (blocks // SPLIT) + line_class
             limits.append(lax.div(offset - key_class + SPLIT, SPLIT) - 1)
+        late_limit, early_limit = limits if u else limits[::-1]
+        taken = early_lanes(lane, slot, per, u)
         is_near = near_tiles(pair, supers, u)
         zero = jnp.zeros((heads, rows), F32)
         parts = [zero, zero, zero, zero]
@@ -203,12 +226,18 @@
             cut = slice(mine + j * rows, mine + (j + 1) * rows)
             squashed = jnp.tanh(squashed_ref[:, cut] / logit_cap)
             weights = jnp.exp(logit_cap * squashed)
-            if j >= supers - 1:
-                weights = jnp.where(lane <= limits[0 if is_near[j] else 1], weights, 0.0)
+            if j == supers - 1:
+                limit = jnp.where(taken, early_limit + rows // 2, late_limit)
+                weights = jnp.where(lane <= limit, weights, 0.0)
+            elif j == supers:
+                limit = jnp.minimum(early_limit, rows // 4 - 1)
+                weights = jnp.where(lane <= limit, weights, 0.0)
             squashed_ref[:, cut] = squashed
             weight_ref[:, cut] = weights
             dots = weights * grad_ref[:, cut]
             near = jnp.where(is_near[j], 1.0, 0.0)
+            if j == supers - 1:
+                near = jnp.where(taken, 1.0 - near, near)
             for n, values in enumerate((weights, dots)):
                 parts[2 * n] += values * near
                 parts[2 * n + 1] += values * (1.0 - near)
@@ -224,14 +253,16 @@
 ):
     supers = blocks // SPLIT
     per = strip * SPLIT // 2
-    pair = lax.div(lax.axis_index(HEAD_AXES), per)
+    own = lax.axis_index(HEAD_AXES)
+    pair, slot = lax.div(own, per), lax.rem(own, per)
     owners = heads // HEADS
     full = supers * rows
     pre, post = pre_ref[...], post_ref[...]
     lane = iota((heads, rows), 1)
     sums = own_ref[...] + other_ref[...]
+    shared = jnp.zeros((heads, rows), F32)
     for u in range(2):
-        base = u * (2 * supers + 1) * rows
+        base = 2 * u * full
         mine = u * (supers + 1) * rows
         near_total, far_total, near_dot, far_dot = [
             jnp.sum(jnp.where(lane == 4 * u + n, sums, 0.0), axis=1, keepdims=True)
@@ -242,25 +273,30 @@
         is_near = near_tiles(pair, supers, u)
         for j in range(supers + 1):
             cut = slice(mine + j * rows, mine + (j + 1) * rows)
-            probs = weight_ref[:, cut] * jnp.where(is_near[j], near_scale, far_scale)
+            here = is_near[j]
+            if j == supers - 1:
+                here = early_lanes(lane, slot, per, u) ^ (u == 1)
+            probs = weight_ref[:, cut] * jnp.where(here, near_scale, far_scale)
             squashed = squashed_ref[:, cut]
-            grad_capped = probs * (grad_ref[:, cut] - jnp.where(is_near[j], near_row, far_row))
+            grad_capped = probs * (grad_ref[:, cut] - jnp.where(here, near_row, far_row))
             both_ref[0, :, cut] = (grad_capped * (1.0 - squashed * squashed)).astype(BF16)
             both_ref[1, :, cut] = probs.astype(BF16)
         cut = slice(mine, mine + full + rows)
         grad_scores = dot(pre, both_ref[0, :, cut], 0, 0) * scaling
         post_mixed = dot(post, both_ref[1, :, cut])
-        joined = jnp.where(
-            lane < rows // 2, grad_scores[:, full:], roll(post_mixed[:, full:], rows // 2)
-        )
+        for kind, values in enumerate((grad_scores, post_mixed)):
+            quarter = 2 * u + kind
+            shared = jnp.where(
+                lane // (rows // 4) == quarter,
+                roll(values[:, full:], quarter * rows // 4),
+                shared,
+            )
         shape = (owners, HEADS, full)
         out_ref[:, :, base : base + full] = grad_scores[:, :full].astype(BF16).reshape(shape)
         out_ref[:, :, base + full : base + 2 * full] = (
             post_mixed[:, :full].astype(BF16).reshape(shape)
         )
-        out_ref[:, :, base + 2 * full : base + 2 * full + rows] = joined.astype(BF16).reshape(
-            owners, HEADS, rows
-        )
+    out_ref[:, :, 4 * full :] = shared.astype(BF16).reshape(owners, HEADS, rows)
 
 
 def grad_kernel(
@@ -272,24 +308,25 @@
     per = strip * SPLIT // 2
     side = per * HEADS
     group = 2 * side
-    tiles = 2 * supers + 1
     part = rows // SPLIT
     sort_blocks(
         block_ref, received_ref, order_ref, key_value_ref, spread_ref, lines_ref, blocks, rows, strip
     )
-    low = iota((side, rows), 1) < rows // 2
+    lane_of = iota((side, rows), 1)
     for c in range(half):
         own = slice(c * per, (c + 1) * per)
+        shared = incoming_ref[own, :, 4 * supers * rows :].reshape(side, rows).astype(F32)
         for u in range(2):
-            lane = (u * tiles + 2 * supers) * rows
-            extra = incoming_ref[own, :, lane : lane + rows].reshape(side, rows).astype(F32)
+            taken = blended(side, rows, u)
             for kind in range(2):
-                base = (u * tiles + kind * supers) * rows
+                base = (2 * u + kind) * supers * rows
                 last = base + (supers - 1) * rows
-                full = incoming_ref[own, :, last : last + rows].reshape(side, rows)
-                rest = extra if kind == 0 else roll(extra, rows // 2)
-                rest = jnp.where(low, rest, 0.0).astype(BF16)
-                near, far = (full, rest) if u else (rest, full)
+                full = incoming_ref[own, :, last : last + rows].reshape(side, rows).astype(F32)
+                late = jnp.where(taken, 0.0, full).astype(BF16)
+                second = roll(jnp.where(taken, full, 0.0), rows // 2)
+                first = roll(shared, -(2 * u + kind) * (rows // 4))
+                early = jnp.where(lane_of < rows // 4, first, second).astype(BF16)
+                near, far = (late, early) if u else (early, late)
                 for p, diagonal, lane in ((c, near, base), (supers - 1 - c, far, base + c * rows)):
                     slots = slice(p * group + u * side, p * group + (u + 1) * side)
                     if p:
@@ -363,7 +400,7 @@
     whole = pl.BlockSpec(memory_space=pltpu.VMEM)
     table = pl.BlockSpec(memory_space=pltpu.SMEM)
     seq_shape = (blocks, rows // SPLIT + strip, 2 * width)
-    head_shape = (owners, HEADS, 2 * (2 * supers + 1) * rows)
+    head_shape = (owners, HEADS, (4 * supers + 1) * rows)
     static = dict(blocks=blocks, rows=rows, strip=strip)
 
     def call(kernel, ins, outs, scratch=(), dtype=BF16, **more):

time: 329 us -> 324 us (0.985)
  blocking collectives: 314 us -> 308 us
    all_to_all x4, blocking collectives: 314 us -> 308 us  [exchange(): lax.all_to_all(values, axes, split_axis=0, concat_axis=0, tiled=True)]
where the time goes in v6:
time: 324 us; the launch traced here: 323 us
  blocking collectives  308 us (95%)
  Pallas kernels  8.03 us (2%)
  waiting for transfers between devices  3.85 us (1%)
    all_to_all x4, blocking collectives, exchange(): lax.all_to_all(values, axes, split_axis=0, concat_axis=0, tiled=True)  308 us
  transfers between devices with their start and end apart: 1, of which 1 were waited for; matrix products, arithmetic and copies ran while one was open for 0% of the time, Pallas kernels for 0%

profile of v6, /device:TPU:32, one launch (start us, length us, event | category | flops | bytes accessed | tf_op | source)
XLA Modules:
  0.0 323.2 jit_solution(13220622240764999869)
XLA Ops:
  0.6 1.2 shard_map.102
  1.9 0.0 copy-start.2
  1.9 26.6 %all_to_all.20.received_ref = bf16[16,80,512]{2,1,0:T(8,128)(2,1)S(1)} all-to-all(bf16[16,80,512]{2,1,0:T(8,128)(2,1)S(1)} %shard_map.102), channel_id=1, replica_groups=mesh['seq'=16,'row'=8,'col'=8] {'seq'}, dimensions={0} | all-to-all | bytes 2621440 | tf_op jit(solution)/shard_map/all_to_all | solution.py:418
  28.4 0.0 copy-done.2
  28.4 1.5 shard_map.103
  29.9 0.0 copy-start
  29.9 0.0 copy-start.1
  29.9 141.3 %all_to_all.21.incoming_ref = bf16[64,2,4224]{2,1,0:T(2,128)(2,1)S(1)} all-to-all(bf16[64,2,4224]{2,1,0:T(2,128)(2,1)S(1)} %shard_map.103), channel_id=1, replica_groups=mesh['seq'=16,'row'=8,'col'=8] {'row','col'}, dimensions={0} | all-to-all | bytes 2162688 | tf_op jit(solution)/shard_map/all_to_all | solution.py:418
  171.3 0.0 copy-done
  171.3 0.0 copy-done.1
  171.3 0.9 shard_map.104
  172.2 2.3 collective-permute-start
  174.5 3.8 %collective-permute-done.other_ref = f32[128,128]{1,0:T(8,128)S(1)} collective-permute-done((f32[128,128]{1,0:T(8,128)S(1)}, f32[128,128]{1,0:T(8,128)S(1)}, u32[]{:S(2)}, u32[]{:S(2)}) %collective-permute-start) | collective-permute-done | bytes 65568 | tf_op jit(solution)/shard_map/ppermute | solution.py:453
  178.4 1.0 shard_map.105
  179.4 117.3 %all_to_all.22.incoming_ref = bf16[64,2,4224]{2,1,0:T(2,128)(2,1)S(1)} all-to-all(bf16[64,2,4224]{2,1,0:T(2,128)(2,1)S(1)} %shard_map.105), channel_id=1, replica_groups=mesh['seq'=16,'row'=8,'col'=8] {'row','col'}, dimensions={0} | all-to-all | bytes 2162688 | tf_op jit(solution)/shard_map/all_to_all | solution.py:418
  296.7 2.4 shard_map.106
  299.1 23.0 %all_to_all.23.received_ref = bf16[16,80,512]{2,1,0:T(8,128)(2,1)S(1)} all-to-all(bf16[16,80,512]{2,1,0:T(8,128)(2,1)S(1)} %shard_map.106), channel_id=1, replica_groups=mesh['seq'=16,'row'=8,'col'=8] {'seq'}, dimensions={0} | all-to-all | bytes 2621440 | tf_op jit(solution)/shard_map/all_to_all | solution.py:418
  322.1 1.0 shard_map.107
Async XLA Ops:
  1.9 26.6 %copy-start.2 = (s32[16]{0:T(128)S(1)}, s32[16]{0:T(128)}, u32[]{:S(2)}) copy-start(s32[16]{0:T(128)} %block_ref.3) | copy-start | bytes 196
  29.9 141.4 %copy-start = (bf16[128,128]{1,0:T(8,128)(2,1)S(1)}, bf16[128,128]{1,0:T(8,128)(2,1)}, u32[]{:S(2)}) copy-start(bf16[128,128]{1,0:T(8,128)(2,1)} %pre_ref.3) | copy-start | bytes 98308
  29.9 141.4 %copy-start.1 = (bf16[128,128]{1,0:T(8,128)(2,1)S(1)}, bf16[128,128]{1,0:T(8,128)(2,1)}, u32[]{:S(2)}) copy-start(bf16[128,128]{1,0:T(8,128)(2,1)} %post_ref.3) | copy-start | bytes 98308
  172.2 6.2 %collective-permute-start = (f32[128,128]{1,0:T(8,128)S(1)}, f32[128,128]{1,0:T(8,128)S(1)}, u32[]{:S(2)}, u32[]{:S(2)}) collective-permute-start(f32[128,128]{1,0:T(8,128)S(1)} %get-tuple-element.11.own_ref), channel_id=1, source_target_pairs={{0,64},{64,0},{128,192},{192,128},{256,320},{320,256},{384,448},{4... | collective-permute-start | bytes 196616 | tf_op jit(solution)/shard_map/ppermute | solution.py:453

commit v7 on v6

--- a/solution.py
+++ b/solution.py
@@ -16,6 +16,7 @@
 HEADS = 2
 CHUNK = 2
 SPLIT = 2
+SUMS = 8
 VMEM_LIMIT = 24 << 20
 INTERP = False
 BF16, F32 = jnp.bfloat16, jnp.float32
@@ -98,7 +99,7 @@
 
 
 def score_kernel(
-    block_ref, received_ref, out_ref, order_ref, key_value_ref, spread_ref, lines_ref, diagonal_ref,
+    block_ref, received_ref, out_ref, key_value_ref, spread_ref, order_ref, lines_ref, diagonal_ref,
     *, blocks, rows, strip, width, scaling
 ):
     supers = blocks // SPLIT
@@ -244,7 +245,7 @@
         for n, values in enumerate(parts):
             down = jnp.sum(values, axis=1, keepdims=True)
             sums += jnp.where(lane == 4 * u + n, down, 0.0)
-    sum_ref[...] = sums
+    sum_ref[...] = jnp.transpose(sums)[:SUMS]
 
 
 def mix_kernel(
@@ -260,6 +261,9 @@
     pre, post = pre_ref[...], post_ref[...]
     lane = iota((heads, rows), 1)
     sums = own_ref[...] + other_ref[...]
+    if rows > SUMS:
+        sums = jnp.concatenate([sums, jnp.zeros((rows - SUMS, heads), F32)], axis=0)
+    sums = jnp.transpose(sums)
     shared = jnp.zeros((heads, rows), F32)
     for u in range(2):
         base = 2 * u * full
@@ -300,8 +304,8 @@
 
 
 def grad_kernel(
-    block_ref, incoming_ref, received_ref, out_ref, dense_ref, sum_ref, order_ref, key_value_ref,
-    spread_ref, lines_ref, *, blocks, rows, strip, width
+    block_ref, incoming_ref, key_value_ref, spread_ref, out_ref, dense_ref, sum_ref, order_ref,
+    *, blocks, rows, strip, width
 ):
     supers = blocks // SPLIT
     half = supers // 2
@@ -309,9 +313,8 @@
     side = per * HEADS
     group = 2 * side
     part = rows // SPLIT
-    sort_blocks(
-        block_ref, received_ref, order_ref, key_value_ref, spread_ref, lines_ref, blocks, rows, strip
-    )
+    for s in range(blocks):
+        order_ref[block_ref[s]] = s
     lane_of = iota((side, rows), 1)
     for c in range(half):
         own = slice(c * per, (c + 1) * per)
@@ -431,23 +434,21 @@
         width=width,
     )(*[far(values) for values in (query_rows, key_rows, value_rows, out_grad)])
     received = exchange(sent, "seq")
-    sorted_blocks = [
-        pltpu.SMEM((blocks,), jnp.int32),
-        pltpu.VMEM((keys, 2 * width), BF16),
-        pltpu.VMEM((slots, 2 * width), BF16),
-        pltpu.VMEM((lines, 2 * width), F32),
-    ]
-    (packed,) = call(
+    packed, key_value, line_rows = call(
         score_kernel,
         [table, whole],
-        [head_shape],
-        sorted_blocks + [pltpu.VMEM((2, supers, HEADS * strip * SPLIT, rows), F32)],
+        [head_shape, (keys, 2 * width), (slots, 2 * width)],
+        [
+            pltpu.SMEM((blocks,), jnp.int32),
+            pltpu.VMEM((lines, 2 * width), F32),
+            pltpu.VMEM((2, supers, HEADS * strip * SPLIT, rows), F32),
+        ],
         width=width, scaling=scaling,
     )(block_order, received)
     weights, squashed, grads, sums = call(
         weigh_kernel,
         [whole] * 3,
-        [(heads, span)] * 3 + [(heads, rows)],
+        [(heads, span)] * 3 + [(SUMS, heads)],
         dtype=F32, heads=heads,
     )(exchange(packed, HEAD_AXES), mix_pre, mix_post)
     others = lax.ppermute(sums, "seq", [(s, s ^ 1) for s in range(blocks)])
@@ -460,11 +461,15 @@
     )(near(weights), near(squashed), near(grads), sums, near(others), mix_pre, mix_post)
     (sent,) = call(
         grad_kernel,
-        [table, whole, whole],
+        [table, whole, whole, whole],
         [seq_shape],
-        [pltpu.VMEM((2, slots, keys), BF16), pltpu.VMEM((slots, width), F32)] + sorted_blocks,
+        [
+            pltpu.VMEM((2, slots, keys), BF16),
+            pltpu.VMEM((slots, width), F32),
+            pltpu.SMEM((blocks,), jnp.int32),
+        ],
         width=width,
-    )(block_order, exchange(mixed, HEAD_AXES), received)
+    )(block_order, exchange(mixed, HEAD_AXES), near(key_value), near(line_rows))
     return call(
         final_kernel,
         [whole],

time: 324 us -> 323 us (level)
  no operation moved by 1% of the time
where the time goes in v7:
time: 323 us
  blocking collectives  308 us (95%)
  Pallas kernels  8.05 us (2%)
    all_to_all x4, blocking collectives, exchange(): lax.all_to_all(values, axes, split_axis=0, concat_axis=0, tiled=True)  308 us
  transfers between devices with their start and end apart: 1, of which 1 were waited for; matrix products, arithmetic and copies ran while one was open for 0% of the time, Pallas kernels for 0%

profile of v7, /device:TPU:32, one launch (start us, length us, event | category | flops | bytes accessed | tf_op | source)
XLA Modules:
  0.0 322.5 jit_solution(17849356242110854675)
XLA Ops:
  0.6 1.2 shard_map.102
  1.9 0.0 copy-start.2
  1.9 26.6 %all_to_all.20.received_ref = bf16[16,80,512]{2,1,0:T(8,128)(2,1)S(1)} all-to-all(bf16[16,80,512]{2,1,0:T(8,128)(2,1)S(1)} %shard_map.102), channel_id=1, replica_groups=mesh['seq'=16,'row'=8,'col'=8] {'seq'}, dimensions={0} | all-to-all | bytes 2621440 | tf_op jit(solution)/shard_map/all_to_all | solution.py:421
  28.4 0.0 copy-done.2
  28.4 1.5 shard_map.103
  29.9 0.0 copy-start
  29.9 0.0 copy-start.1
  29.9 141.4 %all_to_all.21.incoming_ref = bf16[64,2,4224]{2,1,0:T(2,128)(2,1)S(1)} all-to-all(bf16[64,2,4224]{2,1,0:T(2,128)(2,1)S(1)} %get-tuple-element.11), channel_id=1, replica_groups=mesh['seq'=16,'row'=8,'col'=8] {'row','col'}, dimensions={0} | all-to-all | bytes 2162688 | tf_op jit(solution)/shard_map/all_to_all | solution.py:421
  171.3 0.0 copy-done
  171.3 0.0 copy-done.1
  171.3 1.0 shard_map.104
  172.3 2.3 collective-permute-start
  174.6 3.2 collective-permute-done.other_ref
  177.8 1.1 shard_map.105
  178.9 117.3 %all_to_all.22.incoming_ref = bf16[64,2,4224]{2,1,0:T(2,128)(2,1)S(1)} all-to-all(bf16[64,2,4224]{2,1,0:T(2,128)(2,1)S(1)} %shard_map.105), channel_id=1, replica_groups=mesh['seq'=16,'row'=8,'col'=8] {'row','col'}, dimensions={0} | all-to-all | bytes 2162688 | tf_op jit(solution)/shard_map/all_to_all | solution.py:421
  296.2 2.2 shard_map.106
  298.5 23.0 %all_to_all.23.received_ref = bf16[16,80,512]{2,1,0:T(8,128)(2,1)S(1)} all-to-all(bf16[16,80,512]{2,1,0:T(8,128)(2,1)S(1)} %shard_map.106), channel_id=1, replica_groups=mesh['seq'=16,'row'=8,'col'=8] {'seq'}, dimensions={0} | all-to-all | bytes 2621440 | tf_op jit(solution)/shard_map/all_to_all | solution.py:421
  321.5 1.0 shard_map.107
Async XLA Ops:
  1.9 26.6 %copy-start.2 = (s32[16]{0:T(128)S(1)}, s32[16]{0:T(128)}, u32[]{:S(2)}) copy-start(s32[16]{0:T(128)} %block_ref.3) | copy-start | bytes 196
  29.9 141.4 %copy-start = (bf16[128,128]{1,0:T(8,128)(2,1)S(1)}, bf16[128,128]{1,0:T(8,128)(2,1)}, u32[]{:S(2)}) copy-start(bf16[128,128]{1,0:T(8,128)(2,1)} %pre_ref.3) | copy-start | bytes 98308
  29.9 141.4 %copy-start.1 = (bf16[128,128]{1,0:T(8,128)(2,1)S(1)}, bf16[128,128]{1,0:T(8,128)(2,1)}, u32[]{:S(2)}) copy-start(bf16[128,128]{1,0:T(8,128)(2,1)} %post_ref.3) | copy-start | bytes 98308
  172.3 5.5 %collective-permute-start = (f32[8,128]{1,0:T(8,128)S(1)}, f32[8,128]{1,0:T(8,128)S(1)}, u32[]{:S(2)}, u32[]{:S(2)}) collective-permute-start(f32[8,128]{1,0:T(8,128)S(1)} %get-tuple-element.15.own_ref), channel_id=1, source_target_pairs={{0,64},{64,0},{128,192},{192,128},{256,320},{320,256},{384,448},{4... | collective-permute-start | bytes 12296 | tf_op jit(solution)/shard_map/ppermute | solution.py:454

commit v8 on v7

--- a/solution.py
+++ b/solution.py
@@ -13,6 +13,7 @@
 logit_cap = 10.0
 
 HEAD_AXES = ("row", "col")
+OWNER_AXES = ("col", "row")
 HEADS = 2
 CHUNK = 2
 SPLIT = 2
@@ -44,6 +45,15 @@
     block, slot = row // (reach * HEADS), row // HEADS % reach
     line = jnp.where(block < supers // 2, slot, reach - 1 - slot)
     return jnp.where(block * reach + line == column, 1.0, 0.0).astype(BF16)
+
+
+def exchange_order(pre_ref, post_ref, heads, outer):
+    row, column = iota((heads, heads), 0), iota((heads, heads), 1)
+    owner = row // HEADS
+    inner = heads // HEADS // outer
+    stored = (owner % outer * inner + owner // outer) * HEADS + row % HEADS
+    pick = jnp.where(stored == column, 1.0, 0.0).astype(BF16)
+    return dot(pre_ref[...], pick, 1, 1).astype(BF16), dot(pick, post_ref[...]).astype(BF16)
 
 
 def own_head(shape):
@@ -184,15 +194,15 @@
 
 def weigh_kernel(
     incoming_ref, pre_ref, post_ref, weight_ref, squashed_ref, grad_ref, sum_ref,
-    *, blocks, rows, strip, heads
+    *, blocks, rows, strip, heads, outer
 ):
     supers = blocks // SPLIT
     per = strip * SPLIT // 2
-    own = lax.axis_index(HEAD_AXES)
+    own = lax.axis_index(OWNER_AXES)
     pair, slot = lax.div(own, per), lax.rem(own, per)
     seq = lax.axis_index("seq")
     line_class, key_class = lax.div(seq, SPLIT), lax.rem(seq, SPLIT)
-    pre, post = pre_ref[...], post_ref[...]
+    pre, post = exchange_order(pre_ref, post_ref, heads, outer)
     lane = iota((heads, rows), 1)
     full = supers * rows
     sums = jnp.zeros((heads, rows), F32)
@@ -250,15 +260,15 @@
 
 def mix_kernel(
     weight_ref, squashed_ref, grad_ref, own_ref, other_ref, pre_ref, post_ref, out_ref, both_ref,
-    *, blocks, rows, strip, heads, scaling
+    *, blocks, rows, strip, heads, outer, scaling
 ):
     supers = blocks // SPLIT
     per = strip * SPLIT // 2
-    own = lax.axis_index(HEAD_AXES)
+    own = lax.axis_index(OWNER_AXES)
     pair, slot = lax.div(own, per), lax.rem(own, per)
     owners = heads // HEADS
     full = supers * rows
-    pre, post = pre_ref[...], post_ref[...]
+    pre, post = exchange_order(pre_ref, post_ref, heads, outer)
     lane = iota((heads, rows), 1)
     sums = own_ref[...] + other_ref[...]
     if rows > SUMS:
@@ -390,7 +400,8 @@
 
 def body(query_rows, key_rows, value_rows, out_grad, mix_pre, mix_post, block_order):
     blocks = lax.axis_size("seq")
-    owners = lax.axis_size("row") * lax.axis_size("col")
+    outer = lax.axis_size("row")
+    owners = outer * lax.axis_size("col")
     rows, width = query_rows.shape
     heads = mix_pre.shape[0]
     scaling = DH ** (-0.5)
@@ -449,15 +460,15 @@
         weigh_kernel,
         [whole] * 3,
         [(heads, span)] * 3 + [(SUMS, heads)],
-        dtype=F32, heads=heads,
-    )(exchange(packed, HEAD_AXES), mix_pre, mix_post)
+        dtype=F32, heads=heads, outer=outer,
+    )(exchange(packed, OWNER_AXES), mix_pre, mix_post)
     others = lax.ppermute(sums, "seq", [(s, s ^ 1) for s in range(blocks)])
     (mixed,) = call(
         mix_kernel,
         [whole] * 7,
         [head_shape],
         [pltpu.VMEM((2, heads, span), BF16)],
-        heads=heads, scaling=scaling,
+        heads=heads, outer=outer, scaling=scaling,
     )(near(weights), near(squashed), near(grads), sums, near(others), mix_pre, mix_post)
     (sent,) = call(
         grad_kernel,
@@ -469,7 +480,7 @@
             pltpu.SMEM((blocks,), jnp.int32),
         ],
         width=width,
-    )(block_order, exchange(mixed, HEAD_AXES), near(key_value), near(line_rows))
+    )(block_order, exchange(mixed, OWNER_AXES), near(key_value), near(line_rows))
     return call(
         final_kernel,
         [whole],

time: 323 us -> 313 us (0.969)
  the two profiles are of different devices: /device:TPU:32 before, /device:TPU:96 now
where the time goes in v8:
time: 313 us
  blocking collectives  298 us (95%)
  Pallas kernels  8.21 us (3%)
  waiting for transfers between devices  3.2 us (1%)
    all_to_all x4, blocking collectives, exchange(): lax.all_to_all(values, axes, split_axis=0, concat_axis=0, tiled=True)  298 us
  transfers between devices with their start and end apart: 1, of which 1 were waited for; matrix products, arithmetic and copies ran while one was open for 0% of the time, Pallas kernels for 0%

profile of v8, /device:TPU:96, one launch (start us, length us, event | category | flops | bytes accessed | tf_op | source)
XLA Modules:
  0.0 312.9 jit_solution(1694336293688274085)
XLA Ops:
  0.6 1.2 shard_map.102
  1.9 0.0 copy-start.2
  1.9 26.6 %all_to_all.20.received_ref = bf16[16,80,512]{2,1,0:T(8,128)(2,1)S(1)} all-to-all(bf16[16,80,512]{2,1,0:T(8,128)(2,1)S(1)} %shard_map.102), channel_id=1, replica_groups=mesh['seq'=16,'row'=8,'col'=8] {'seq'}, dimensions={0} | all-to-all | bytes 2621440 | tf_op jit(solution)/shard_map/all_to_all | solution.py:432
  28.4 0.0 copy-done.2
  28.4 1.5 shard_map.103
  29.9 0.0 copy-start
  29.9 0.0 copy-start.1
  29.9 137.4 %all_to_all.21.incoming_ref = bf16[64,2,4224]{2,1,0:T(2,128)(2,1)S(1)} all-to-all(bf16[64,2,4224]{2,1,0:T(2,128)(2,1)S(1)} %get-tuple-element.11), channel_id=1, replica_groups=mesh['seq'=16,'row'=8,'col'=8] {'col','row'}, dimensions={0} | all-to-all | bytes 2162688 | tf_op jit(solution)/shard_map/all_to_all | solution.py:432
  167.4 0.0 copy-done
  167.4 0.0 copy-done.1
  167.4 1.1 shard_map.104
  168.5 2.3 collective-permute-start
  170.8 3.2 %collective-permute-done.other_ref = f32[8,128]{1,0:T(8,128)S(1)} collective-permute-done((f32[8,128]{1,0:T(8,128)S(1)}, f32[8,128]{1,0:T(8,128)S(1)}, u32[]{:S(2)}, u32[]{:S(2)}) %collective-permute-start) | collective-permute-done | bytes 4128 | tf_op jit(solution)/shard_map/ppermute | solution.py:465
  174.0 1.2 shard_map.105
  175.2 116.1 %all_to_all.22.incoming_ref = bf16[64,2,4224]{2,1,0:T(2,128)(2,1)S(1)} all-to-all(bf16[64,2,4224]{2,1,0:T(2,128)(2,1)S(1)} %shard_map.105), channel_id=1, replica_groups=mesh['seq'=16,'row'=8,'col'=8] {'col','row'}, dimensions={0} | all-to-all | bytes 2162688 | tf_op jit(solution)/shard_map/all_to_all | solution.py:432
  291.2 2.2 shard_map.106
  293.4 18.4 %all_to_all.23.received_ref = bf16[16,80,512]{2,1,0:T(8,128)(2,1)S(1)} all-to-all(bf16[16,80,512]{2,1,0:T(8,128)(2,1)S(1)} %shard_map.106), channel_id=1, replica_groups=mesh['seq'=16,'row'=8,'col'=8] {'seq'}, dimensions={0} | all-to-all | bytes 2621440 | tf_op jit(solution)/shard_map/all_to_all | solution.py:432
  311.8 1.0 shard_map.107
Async XLA Ops:
  1.9 26.6 %copy-start.2 = (s32[16]{0:T(128)S(1)}, s32[16]{0:T(128)}, u32[]{:S(2)}) copy-start(s32[16]{0:T(128)} %block_ref.3) | copy-start | bytes 196
  29.9 137.4 %copy-start = (bf16[128,128]{1,0:T(8,128)(2,1)S(1)}, bf16[128,128]{1,0:T(8,128)(2,1)}, u32[]{:S(2)}) copy-start(bf16[128,128]{1,0:T(8,128)(2,1)} %pre_ref.3) | copy-start | bytes 98308
  29.9 137.4 %copy-start.1 = (bf16[128,128]{1,0:T(8,128)(2,1)S(1)}, bf16[128,128]{1,0:T(8,128)(2,1)}, u32[]{:S(2)}) copy-start(bf16[128,128]{1,0:T(8,128)(2,1)} %post_ref.3) | copy-start | bytes 98308
  168.5 5.5 %collective-permute-start = (f32[8,128]{1,0:T(8,128)S(1)}, f32[8,128]{1,0:T(8,128)S(1)}, u32[]{:S(2)}, u32[]{:S(2)}) collective-permute-start(f32[8,128]{1,0:T(8,128)S(1)} %get-tuple-element.15.own_ref), channel_id=1, source_target_pairs={{0,64},{64,0},{128,192},{192,128},{256,320},{320,256},{384,448},{4... | collective-permute-start | bytes 12296 | tf_op jit(solution)/shard_map/ppermute | solution.py:465

commit v9 on v8

--- a/solution.py
+++ b/solution.py
@@ -15,7 +15,7 @@
 HEAD_AXES = ("row", "col")
 OWNER_AXES = ("col", "row")
 HEADS = 2
-CHUNK = 2
+CHUNK = 4
 SPLIT = 2
 SUMS = 8
 VMEM_LIMIT = 24 << 20

time: 313 us -> 313 us (level)
  no operation moved by 1% of the time
where the time goes in v9:
time: 313 us
  blocking collectives  298 us (95%)
  Pallas kernels  8.12 us (3%)
  waiting for transfers between devices  3.19 us (1%)
    all_to_all x4, blocking collectives, exchange(): lax.all_to_all(values, axes, split_axis=0, concat_axis=0, tiled=True)  298 us
  transfers between devices with their start and end apart: 1, of which 1 were waited for; matrix products, arithmetic and copies ran while one was open for 0% of the time, Pallas kernels for 0%

profile of v9, /device:TPU:96, one launch (start us, length us, event | category | flops | bytes accessed | tf_op | source)
XLA Modules:
  0.0 312.8 jit_solution(13433773586289009016)
XLA Ops:
  0.6 1.2 shard_map.102
  1.9 0.0 copy-start.2
  1.9 26.6 %all_to_all.20.received_ref = bf16[16,80,512]{2,1,0:T(8,128)(2,1)S(1)} all-to-all(bf16[16,80,512]{2,1,0:T(8,128)(2,1)S(1)} %shard_map.102), channel_id=1, replica_groups=mesh['seq'=16,'row'=8,'col'=8] {'seq'}, dimensions={0} | all-to-all | bytes 2621440 | tf_op jit(solution)/shard_map/all_to_all | solution.py:432
  28.4 0.0 copy-done.2
  28.4 1.4 shard_map.103
  29.9 0.0 copy-start
  29.9 0.0 copy-start.1
  29.9 137.4 %all_to_all.21.incoming_ref = bf16[64,2,4224]{2,1,0:T(2,128)(2,1)S(1)} all-to-all(bf16[64,2,4224]{2,1,0:T(2,128)(2,1)S(1)} %get-tuple-element.11), channel_id=1, replica_groups=mesh['seq'=16,'row'=8,'col'=8] {'col','row'}, dimensions={0} | all-to-all | bytes 2162688 | tf_op jit(solution)/shard_map/all_to_all | solution.py:432
  167.3 0.0 copy-done
  167.3 0.0 copy-done.1
  167.3 1.1 shard_map.104
  168.4 2.3 collective-permute-start
  170.7 3.2 %collective-permute-done.other_ref = f32[8,128]{1,0:T(8,128)S(1)} collective-permute-done((f32[8,128]{1,0:T(8,128)S(1)}, f32[8,128]{1,0:T(8,128)S(1)}, u32[]{:S(2)}, u32[]{:S(2)}) %collective-permute-start) | collective-permute-done | bytes 4128 | tf_op jit(solution)/shard_map/ppermute | solution.py:465
  173.9 1.2 shard_map.105
  175.1 116.1 %all_to_all.22.incoming_ref = bf16[64,2,4224]{2,1,0:T(2,128)(2,1)S(1)} all-to-all(bf16[64,2,4224]{2,1,0:T(2,128)(2,1)S(1)} %shard_map.105), channel_id=1, replica_groups=mesh['seq'=16,'row'=8,'col'=8] {'col','row'}, dimensions={0} | all-to-all | bytes 2162688 | tf_op jit(solution)/shard_map/all_to_all | solution.py:432
  291.2 2.2 shard_map.106
  293.3 18.4 %all_to_all.23.received_ref = bf16[16,80,512]{2,1,0:T(8,128)(2,1)S(1)} all-to-all(bf16[16,80,512]{2,1,0:T(8,128)(2,1)S(1)} %shard_map.106), channel_id=1, replica_groups=mesh['seq'=16,'row'=8,'col'=8] {'seq'}, dimensions={0} | all-to-all | bytes 2621440 | tf_op jit(solution)/shard_map/all_to_all | solution.py:432
  311.7 1.0 shard_map.107
Async XLA Ops:
  1.9 26.6 %copy-start.2 = (s32[16]{0:T(128)S(1)}, s32[16]{0:T(128)}, u32[]{:S(2)}) copy-start(s32[16]{0:T(128)} %block_ref.3) | copy-start | bytes 196
  29.9 137.4 %copy-start = (bf16[128,128]{1,0:T(8,128)(2,1)S(1)}, bf16[128,128]{1,0:T(8,128)(2,1)}, u32[]{:S(2)}) copy-start(bf16[128,128]{1,0:T(8,128)(2,1)} %pre_ref.3) | copy-start | bytes 98308
  29.9 137.4 %copy-start.1 = (bf16[128,128]{1,0:T(8,128)(2,1)S(1)}, bf16[128,128]{1,0:T(8,128)(2,1)}, u32[]{:S(2)}) copy-start(bf16[128,128]{1,0:T(8,128)(2,1)} %post_ref.3) | copy-start | bytes 98308
  168.4 5.5 %collective-permute-start = (f32[8,128]{1,0:T(8,128)S(1)}, f32[8,128]{1,0:T(8,128)S(1)}, u32[]{:S(2)}, u32[]{:S(2)}) collective-permute-start(f32[8,128]{1,0:T(8,128)S(1)} %get-tuple-element.15.own_ref), channel_id=1, source_target_pairs={{0,64},{64,0},{128,192},{192,128},{256,320},{320,256},{384,448},{4... | collective-permute-start | bytes 12296 | tf_op jit(solution)/shard_map/ppermute | solution.py:465
